TPU v7x, 32 devices: a whole 2x2x4 slice. The times are simulated.
32 devices in a mesh: head: 2 (over x), expert: 16 (over z, y, core).
Axes of the slice: x: 2, y: 2, z: 4, core: 2. Of those that a mesh axis runs over, the one named last changes fastest.
Arguments:
- queries: bfloat16 [256, 128, 576], P('expert', 'head'), may hold values from -64 to 64
- resident_cache: bfloat16 [64, 256, 576], P('expert'), may hold values from -6 to 6
- resident_len: int32 [64], P('expert'), may hold values from 1 to 256, as said below
- new_cache: bfloat16 [192, 64, 576], P('expert'), may hold values from -6 to 6
- new_len: int32 [192], replicated, may hold values from 1 to 64, as said below
- new_owner: int32 [192], replicated, may hold values from 0 to 15, as said below
- value_up: bfloat16 [128, 512, 128], P('head'), may hold values from -0.25 to 0.25
- w_output: bfloat16 [16384, 7168], P('head', 'expert'), may hold values from -0.046875 to 0.046875
- residual: bfloat16 [256, 7168], P(None, 'expert'), may hold values from -6 to 6
- expert_ids: int32 [256, 8], replicated, may hold values from 0 to 15, all different within a row; in each aligned block of 16 rows (0 to 15, 16 to 31, ...) at most 12 rows name the same one
- expert_gates: float32 [256, 8], replicated, may hold values from 0.1 to 1
- norm_gain: bfloat16 [7168], replicated, may hold values from 0.5 to 1.5
- w_gate: bfloat16 [16, 7168, 1024], P('expert', None, 'head'), may hold values from -0.0625 to 0.0625
- w_up: bfloat16 [16, 7168, 1024], P('expert', None, 'head'), may hold values from -0.0625 to 0.0625
- w_down: bfloat16 [16, 1024, 7168], P('expert', 'head'), may hold values from -0.1875 to 0.1875
Outputs:
- layer_out: bfloat16 [256, 7168], P('head', 'expert')
Inputs may be any that keep to these rules, and one draw needn't show every extreme that they name: `resident_len`: every decode owner has a resident request of length 256. `new_len`: every prefill device holds a new request of length 64. `new_owner`: one prefill device sends at most 2 of its 12 new requests to one decode owner, and every decode owner receives exactly 12 in all; a prefill device sends either 2 or none to each owner, except to at most one owner, which gets the remainder of 12 divided by 2. `expert_ids`: in each aligned block of 16 rows (the rows of one decode owner) no expert is named by more than 12 rows; the 8 experts of a row differ.
All inputs are finite; a program needn't handle non-finite values.
Results may differ from a plain program's by a relative error of at most 0.012.
Values may be sent and summed in bfloat16 or wider, within the bound.
A program may use at most 128 MiB of HBM per device.

v0:
```python
import jax
import jax.numpy as jnp
from jax import lax
from jax.sharding import PartitionSpec as P

ROPE = 64
NOPE = 128


def attend(queries, caches, length, value_up):
    inverse_root = (NOPE + ROPE) ** (-0.5)
    latent_width = value_up.shape[1]
    scores = (
        jnp.einsum("rhc,rtc->rht", queries, caches, preferred_element_type=jnp.float32)
        * inverse_root
    )
    inside = lax.broadcasted_iota(jnp.int32, scores.shape, 2) < length[:, None, None]
    scores = jnp.where(inside, scores, -jnp.inf)
    highest = jnp.max(scores, axis=2, keepdims=True)
    raised = jnp.exp(scores - highest)
    weights = (raised / jnp.sum(raised, axis=2, keepdims=True)).astype(jnp.bfloat16)
    latent = jnp.einsum(
        "rht,rtc->rhc", weights, caches[:, :, :latent_width], preferred_element_type=jnp.float32
    ).astype(jnp.bfloat16)
    values = jnp.einsum(
        "rhc,hcv->rhv", latent, value_up, preferred_element_type=jnp.float32
    ).astype(jnp.bfloat16)
    return values.reshape(values.shape[0], -1)


def earlier_equal(labels):
    count = labels.shape[0]
    position = jnp.arange(count, dtype=jnp.int32)
    before = (labels[:, None] == labels[None, :]) & (position[None, :] < position[:, None])
    return jnp.sum(before.astype(jnp.int32), axis=1)


def per_device(
    queries,
    resident_cache,
    resident_len,
    new_cache,
    new_len,
    new_owner,
    value_up,
    w_output,
    residual,
    expert_ids,
    expert_gates,
    norm_gain,
    w_gate,
    w_up,
    w_down,
):
    n_expert = lax.axis_size("expert")
    n_head = lax.axis_size("head")
    owner_index = lax.axis_index("expert")
    head_index = lax.axis_index("head")
    req_count = resident_cache.shape[0]
    new_count, new_span, cache_width = new_cache.shape
    rows_dev = req_count + new_count
    rows_all = rows_dev * n_expert
    local_experts = w_gate.shape[0]
    most = max(2, (4 * new_count + 3 * n_expert - 1) // (3 * n_expert))
    block_rows = rows_all // n_head
    piece = new_span // n_head

    targets = lax.dynamic_slice_in_dim(new_owner, owner_index * new_count, new_count)
    places = targets * most + earlier_equal(targets)
    slots = jnp.arange(n_expert * most, dtype=jnp.int32)
    senders = jnp.sum(
        jnp.where(
            places[None, :] == slots[:, None], jnp.arange(new_count, dtype=jnp.int32)[None, :], 0
        ),
        axis=1,
    )
    share = lax.dynamic_slice_in_dim(new_cache, head_index * piece, piece, axis=1)
    outgoing = jnp.take(share, senders, axis=0, mode="clip").reshape(
        n_expert, most, piece, cache_width
    )
    incoming = lax.all_to_all(outgoing, "expert", split_axis=0, concat_axis=0, tiled=True)
    position = jnp.arange(new_owner.shape[0], dtype=jnp.int32)
    named = new_owner == owner_index
    before = jnp.sum((named[None, :] & (position[None, :] < position[:, None])).astype(jnp.int32), 1)
    chosen = jnp.sum(
        jnp.where(
            named[None, :]
            & (before[None, :] == jnp.arange(new_count, dtype=jnp.int32)[:, None]),
            position[None, :],
            0,
        ),
        axis=1,
    )
    anchor = chosen // new_count
    arrived_share = jnp.take(
        incoming.reshape(n_expert * most, piece, cache_width),
        anchor * most + earlier_equal(anchor),
        axis=0,
        mode="clip",
    )
    arrived = lax.all_gather(arrived_share, "head", axis=1, tiled=True)
    resident_att = attend(queries[:req_count], resident_cache, resident_len, value_up)
    arrived_att = attend(queries[req_count:], arrived, new_len[chosen], value_up)
    attention = jnp.concatenate([resident_att, arrived_att], axis=0)
    mixed = jnp.dot(
        lax.all_gather(attention, "expert", axis=0, tiled=True),
        w_output,
        preferred_element_type=jnp.float32,
    ).T
    swap = [(0, 1), (1, 0)]
    if n_head == 2:
        mixed = mixed.astype(jnp.bfloat16)
        summed = mixed.astype(jnp.float32) + lax.ppermute(mixed, "head", swap).astype(jnp.float32)
    else:
        summed = lax.psum(mixed, "head")
    hidden = (residual.T.astype(jnp.float32) + summed).astype(jnp.bfloat16)
    hidden_block = lax.dynamic_slice_in_dim(hidden, head_index * block_rows, block_rows, axis=1)

    inputs = lax.all_gather(hidden, "expert", axis=0, tiled=True).astype(jnp.float32)
    inverse = lax.rsqrt(jnp.mean(inputs * inputs, axis=0, keepdims=True) + 1e-06)
    normed = (inputs * inverse * norm_gain.astype(jnp.float32)[:, None]).astype(jnp.bfloat16)
    partial = None
    for e in range(local_experts):
        gate_act = jnp.einsum("df,dr->fr", w_gate[e], normed, preferred_element_type=jnp.float32)
        up_act = jnp.einsum("df,dr->fr", w_up[e], normed, preferred_element_type=jnp.float32)
        act = (jax.nn.silu(gate_act) * up_act).astype(jnp.bfloat16)
        down = jnp.einsum("fd,fr->dr", w_down[e], act, preferred_element_type=jnp.float32)
        mine = expert_ids == owner_index * local_experts + e
        weight = jnp.sum(jnp.where(mine, expert_gates, 0.0), axis=1)
        term = down * weight[None, :]
        partial = term if partial is None else partial + term
    routed = lax.psum_scatter(
        partial.astype(jnp.bfloat16), "expert", scatter_dimension=0, tiled=True
    )
    if n_head == 2:
        kept = lax.dynamic_slice_in_dim(routed, head_index * block_rows, block_rows, axis=1)
        sent = lax.dynamic_slice_in_dim(routed, (1 - head_index) * block_rows, block_rows, axis=1)
        got = lax.ppermute(sent, "head", swap)
        routed_block = kept.astype(jnp.float32) + got.astype(jnp.float32)
    else:
        routed_block = lax.psum_scatter(
            routed, "head", scatter_dimension=1, tiled=True
        ).astype(jnp.float32)
    return (hidden_block.astype(jnp.float32) + routed_block).astype(jnp.bfloat16).T


def solution(mesh):
    return jax.shard_map(
        per_device,
        mesh=mesh,
        in_specs=(
            P("expert", "head", None),
            P("expert", None, None),
            P("expert"),
            P("expert", None, None),
            P(),
            P(),
            P("head", None, None),
            P("head", "expert"),
            P(None, "expert"),
            P(),
            P(),
            P(),
            P("expert", None, "head"),
            P("expert", None, "head"),
            P("expert", "head", None),
        ),
        out_specs=P("head", "expert"),
        check_vma=False,
    )
```

profile of v0, /device:TPU:0, one launch (start us, length us, event | category | flops | bytes accessed | tf_op | source)
XLA Modules:
  0.0 290.6 jit_solution(2620647868807348800)
XLA Ops:
  8.5 1.8 gather_fusion.1
  10.2 7.4 %all-to-all-start = ((bf16[16,2,32,576]{3,2,1,0:T(8,128)(2,1)}), bf16[16,2,32,576]{3,2,1,0:T(8,128)(2,1)S(1)}, u32[]{:S(2)}, u32[]{:S(2)}) async-start(bf16[16,2,32,576]{3,2,1,0:T(8,128)(2,1)} %bitcast.5), calls=%async_computation | async-start | bytes 2621440 | tf_op jit(solution)/shard_map/all_to_all | solution.py:81
  18.9 1.3 gather_fusion
  20.2 1.7 fusion.33
  22.1 1.8 convolution_convert_fusion.2
  23.9 4.6 %fusion.35 = bf16[4,8192]{1,0:T(4,128)(2,1)S(1)} fusion(bf16[64,512,128]{2,1,0:T(8,128)(2,1)} %param.21, bf16[4,64,512]{2,1,0:T(8,128)(2,1)S(1)} %convolution_convert_fusion.2), kind=kOutput, calls=%fused_computation.38 | convolution fusion | flops 33587200 | bytes 8716288 | tf_op jit(solution)/shard_map/rhc,hcv->rhv/dot_general | solution.py:25
  28.5 16.5 %all-to-all-done = bf16[16,2,32,576]{3,2,1,0:T(8,128)(2,1)S(1)} async-done(((bf16[16,2,32,576]{3,2,1,0:T(8,128)(2,1)}), bf16[16,2,32,576]{3,2,1,0:T(8,128)(2,1)S(1)}, u32[]{:S(2)}, u32[]{:S(2)}) %all-to-all-start) | async-done | bytes 1179680 | tf_op jit(solution)/shard_map/all_to_all | solution.py:81
  45.6 14.8 %all-gather = bf16[12,64,576]{2,1,0:T(8,128)(2,1)S(1)} all-gather(bf16[12,32,576]{2,1,0:T(8,128)(2,1)S(1)} %gather_fusion.2), channel_id=2, replica_groups=mesh['head'=2,'expert'=16] {'head'}, dimensions={1}, use_global_device_ids=true | all-gather | bytes 1327104 | tf_op jit(solution)/shard_map/all_gather | solution.py:101
  60.4 2.0 fusion.25
  62.5 1.6 convolution_convert_fusion
  64.1 4.8 %fusion.32 = bf16[12,64,128]{2,0,1:T(8,128)(2,1)S(1)} fusion(bf16[64,512,128]{2,1,0:T(8,128)(2,1)} %param.21, bf16[12,64,512]{2,1,0:T(8,128)(2,1)S(1)} %convolution_convert_fusion), kind=kOutput, calls=%fused_computation.33 | convolution fusion | flops 100761600 | bytes 9371648 | tf_op jit(solution)/shard_map/rhc,hcv->rhv/dot_general | solution.py:25
  70.1 53.2 %all-gather.4.cloned.1.call-done = bf16[256,8192]{1,0:T(8,128)(2,1)} async-done(((bf16[16,8192]{1,0:T(8,128)(2,1)}), bf16[256,8192]{1,0:T(8,128)(2,1)}) %all-gather.4.cloned.1.call-update) | async-done | bytes 4194320 | tf_op jit(solution)/shard_map/all_gather | solution.py:106
  123.3 6.4 %fusion.34 = bf16[448,256]{1,0:T(8,128)(2,1)S(1)} fusion(bf16[256,8192]{1,0:T(8,128)(2,1)} %all-gather.4.cloned.1.call-done, bf16[8192,448]{0,1:T(8,128)(2,1)} %param.22), kind=kOutput, calls=%fused_computation.36 | convolution fusion | flops 1879162880 | bytes 11763712 | tf_op jit(solution)/shard_map/dot_general | solution.py:105
  129.7 1.5 collective-permute-start
  131.3 6.3 %collective-permute-done = bf16[448,256]{1,0:T(8,128)(2,1)S(1)} collective-permute-done((bf16[448,256]{1,0:T(8,128)(2,1)S(1)}, bf16[448,256]{1,0:T(8,128)(2,1)S(1)}, u32[]{:S(2)}, u32[]{:S(2)}) %collective-permute-start) | collective-permute-done | bytes 229408 | tf_op jit(solution)/shard_map/ppermute | solution.py:113
  138.6 46.0 %all-gather.6.cloned.1.call-done = bf16[7168,256]{1,0:T(8,128)(2,1)} async-done(((bf16[448,256]{1,0:T(8,128)(2,1)}), bf16[7168,256]{1,0:T(8,128)(2,1)}) %all-gather.6.cloned.1.call-update) | async-done | bytes 3670032 | tf_op jit(solution)/shard_map/all_gather | solution.py:119
  184.7 3.0 %fusion.4 = f32[256]{0:T(256)S(1)} fusion(bf16[7168,256]{1,0:T(8,128)(2,1)} %all-gather.6.cloned.1.call-done), kind=kLoop, calls=%fused_computation.10 | loop fusion | flops 5504768 | bytes 3671040 | tf_op jit(solution)/shard_map/reduce_sum | solution.py:120
  187.7 8.3 %fusion.13 = f32[512,256]{0,1:T(8,128)S(1)} fusion(bf16[1,7168,512]{2,1,0:T(8,128)(2,1)} %param.27, bf16[7168,256]{1,0:T(8,128)(2,1)} %all-gather.6.cloned.1.call-done, f32[7168]{0:T(1024)S(1)} %convert_element_type.104, f32[256]{0:T(256)S(1)} %add_rsqrt_fusion), kind=kOutput, calls=%fused_computation.20 | convolution fusion | flops 1886388224 | bytes 11564032 | tf_op jit(solution)/shard_map/df,dr->fr/dot_general | solution.py:124
  196.0 13.2 %fusion.3 = bf16[7168,256]{1,0:T(8,128)(2,1)} fusion(bf16[1,512,7168]{2,1,0:T(8,128)(2,1)} %param.29, f32[256]{0:T(256)S(1)} %select_reduce_fusion.1, bf16[1,7168,512]{2,1,0:T(8,128)(2,1)} %param.28, bf16[7168,256]{1,0:T(8,128)(2,1)} %all-gather.6.cloned.1.call-done, f32[7168]{0:T(1024)S(1)} %convert_element_type.104, f32[256]{0:T(256)S(1)} %add_rsqrt_fusion, ...), kind=kOutput, calls=%fused_computation.9 | convolution fusion | flops 3769892864 | bytes 22575104 | tf_op jit(solution)/shard_map/fd,fr->dr/dot_general | solution.py:127
  209.3 67.5 %reduce-scatter.2.cloned.1.call-done = bf16[448,256]{1,0:T(8,128)(2,1)} async-done(((bf16[7168,256]{1,0:T(8,128)(2,1)}), bf16[448,256]{1,0:T(8,128)(2,1)}) %reduce-scatter.2.cloned.1.call-update) | async-done | bytes 229392 | tf_op jit(solution)/shard_map/reduce_scatter | solution.py:132
  276.8 0.9 constant_dynamic-slice_fusion
  277.7 1.4 collective-permute-start.1
  279.1 3.4 %collective-permute-done.1 = bf16[448,128]{1,0:T(8,128)(2,1)S(1)} collective-permute-done((bf16[448,128]{1,0:T(8,128)(2,1)S(1)}, bf16[448,128]{1,0:T(8,128)(2,1)S(1)}, u32[]{:S(2)}, u32[]{:S(2)}) %collective-permute-start.1) | collective-permute-done | bytes 114720 | tf_op jit(solution)/shard_map/ppermute | solution.py:138
  282.5 1.6 fusion.54
  (45 shorter events, 6.3 us)
Async XLA Ops:
  6.5 1.9 copy-start
  10.2 34.7 %all-to-all-start = ((bf16[16,2,32,576]{3,2,1,0:T(8,128)(2,1)}), bf16[16,2,32,576]{3,2,1,0:T(8,128)(2,1)S(1)}, u32[]{:S(2)}, u32[]{:S(2)}) async-start(bf16[16,2,32,576]{3,2,1,0:T(8,128)(2,1)} %bitcast.5), calls=%async_computation | async-start | bytes 2621440 | tf_op jit(solution)/shard_map/all_to_all | solution.py:81
  17.7 105.6 %all-gather.4.cloned.1.call-start = ((), (), s32[]{:S(2)}) async-start(), calls=%async_computation.2 | async-start | bytes 4456448 | tf_op jit(solution)/shard_map/all_gather | solution.py:106
  60.4 2.0 copy-start.2
  70.0 67.6 %copy-start.3 = (bf16[256,448]{0,1:T(8,128)(2,1)S(1)}, bf16[256,448]{0,1:T(8,128)(2,1)}, u32[]{:S(2)}) copy-start(bf16[256,448]{0,1:T(8,128)(2,1)} %param.23) | copy-start | bytes 688132
  70.0 68.6 %copy-start.4 = (bf16[7168]{0:T(1024)(128)(2,1)S(1)}, bf16[7168]{0:T(1024)(128)(2,1)}, u32[]{:S(2)}) copy-start(bf16[7168]{0:T(1024)(128)(2,1)} %param.26) | copy-start | bytes 43012
  70.0 68.6 %copy-start.5 = (f32[256,8]{0,1:T(8,128)S(1)}, f32[256,8]{0,1:T(8,128)}, u32[]{:S(2)}) copy-start(f32[256,8]{0,1:T(8,128)} %param.25) | copy-start | bytes 24580
  70.0 68.6 %copy-start.6 = (s32[256,8]{0,1:T(8,128)S(1)}, s32[256,8]{0,1:T(8,128)}, u32[]{:S(2)}) copy-start(s32[256,8]{0,1:T(8,128)} %param.24) | copy-start | bytes 24580
  70.0 114.6 %all-gather.6.cloned.1.call-start = ((), (), s32[]{:S(2)}) async-start(), calls=%async_computation.3 | async-start | bytes 3899392 | tf_op jit(solution)/shard_map/all_gather | solution.py:119
  129.7 7.8 %collective-permute-start = (bf16[448,256]{1,0:T(8,128)(2,1)S(1)}, bf16[448,256]{1,0:T(8,128)(2,1)S(1)}, u32[]{:S(2)}, u32[]{:S(2)}) collective-permute-start(bf16[448,256]{1,0:T(8,128)(2,1)S(1)} %fusion.34), channel_id=1, source_target_pairs={{0,16},{16,0},{1,17},{17,1},{2,18},{18,2},{3,19},{19,3},{4,20},{20... | collective-permute-start | bytes 688136 | tf_op jit(solution)/shard_map/ppermute | solution.py:113
  138.4 138.4 %reduce-scatter.2.cloned.1.call-start = ((), (), s32[]{:S(2)}) async-start(), calls=%async_computation.4 | async-start | bytes 3899392 | tf_op jit(solution)/shard_map/reduce_scatter | solution.py:132
  196.0 86.4 %copy-start.1 = (bf16[448,256]{1,0:T(8,128)(2,1)S(1)}, bf16[448,256]{1,0:T(8,128)(2,1)}, u32[]{:S(2)}) copy-start(bf16[448,256]{1,0:T(8,128)(2,1)} %fusion.48) | copy-start | bytes 688132
  277.7 4.8 %collective-permute-start.1 = (bf16[448,128]{1,0:T(8,128)(2,1)S(1)}, bf16[448,128]{1,0:T(8,128)(2,1)S(1)}, u32[]{:S(2)}, u32[]{:S(2)}) collective-permute-start(bf16[448,128]{1,0:T(8,128)(2,1)S(1)} %constant_dynamic-slice_fusion), channel_id=1, source_target_pairs={{0,16},{16,0},{1,17},{17,1},{2,18},{18,2},{3,19},{19,3},{4,20},{20... | collective-permute-start | bytes 344072 | tf_op jit(solution)/shard_map/ppermute | solution.py:138
Sparse Core Ops, SparseCore 0:
  70.1 53.1 all-gather.3
  138.5 46.1 all-gather.5
  209.4 67.3 reduce-scatter.1
where the time goes:
time: 291 us
  waiting for transfers between devices  193 us (66%)
  matrix products  44.4 us (15%)
  blocking collectives  14.8 us (5%)
  between operations  13.3 us (5%)
  starting transfers between devices  10.7 us (4%)
  other arithmetic  8.7 us (3%)
  local copies, waits for them, and re-layouts  5.83 us (2%)
    reduce_scatter x1, waiting for transfers between devices, per_device(): lax.psum_scatter(partial.astype(jnp.bfloat16), 'expert', scatter_dimensio...  67.5 us
    all_gather x1, waiting for transfers between devices, per_device(): lax.all_gather(attention, 'expert', axis=0, tiled=True)  53.2 us
    all_gather x1, waiting for transfers between devices, per_device(): lax.all_gather(hidden, 'expert', axis=0, tiled=True).astype(jnp.float32)  46 us
    all_to_all x1, waiting for transfers between devices, per_device(): lax.all_to_all(outgoing, 'expert', split_axis=0, concat_axis=0, tiled=True)  16.5 us
    all_gather x1, blocking collectives, per_device(): arrived = lax.all_gather(arrived_share, 'head', axis=1, tiled=True)  14.8 us
    dot_general x1, matrix products, per_device(): jnp.einsum('fd,fr->dr', w_down[e], act, preferred_element_type=jnp.float32)  13.2 us
    dot_general x2, matrix products, attend(): jnp.einsum('rhc,hcv->rhv', latent, value_up, preferred_element_type=jnp.f...  9.42 us
    dot_general x1, matrix products, per_device(): jnp.einsum('df,dr->fr', w_gate[e], normed, preferred_element_type=jnp.flo...  8.31 us
  transfers between devices with their start and end apart: 6, of which 6 were waited for; matrix products, arithmetic and copies ran while one was open for 4% of the time, Pallas kernels for 0%

commit v1 on v0

--- a/solution.py
+++ b/solution.py
@@ -1,10 +1,15 @@
+import functools
+
 import jax
 import jax.numpy as jnp
 from jax import lax
+from jax.experimental import pallas as pl
+from jax.experimental.pallas import tpu as pltpu
 from jax.sharding import PartitionSpec as P
 
 ROPE = 64
 NOPE = 128
+MESH = pl.DeviceIdType.MESH
 
 
 def attend(queries, caches, length, value_up):
@@ -33,6 +38,550 @@
     position = jnp.arange(count, dtype=jnp.int32)
     before = (labels[:, None] == labels[None, :]) & (position[None, :] < position[:, None])
     return jnp.sum(before.astype(jnp.int32), axis=1)
+
+
+class Place:
+    def __init__(self, nz):
+        self.nz = nz
+        self.h = lax.axis_index("head")
+        self.e = lax.axis_index("expert")
+        self.z = self.e // 4
+        self.y = (self.e // 2) % 2
+        self.c = self.e % 2
+
+    def at(self, z, y, c):
+        return z * 4 + y * 2 + c
+
+    def core(self):
+        return (self.h, self.at(self.z, self.y, 1 - self.c))
+
+    def across(self):
+        return (self.h, self.at(self.z, 1 - self.y, self.c))
+
+    def along(self, sign):
+        return (self.h, self.at(self.z + sign, self.y, self.c))
+
+    def other_head(self):
+        return (1 - self.h, self.e)
+
+    def inside(self, z):
+        return (z >= 0) & (z < self.nz)
+
+
+def greet(place):
+    barrier = pltpu.get_barrier_semaphore()
+    for target in (place.core(), place.across(), place.other_head()):
+        pl.semaphore_signal(barrier, inc=1, device_id=target, device_id_type=MESH)
+    for sign in (-1, 1):
+
+        @pl.when(place.inside(place.z + sign))
+        def _():
+            pl.semaphore_signal(
+                barrier, inc=1, device_id=place.along(sign), device_id_type=MESH
+            )
+
+    above = jnp.where(place.z < place.nz - 1, 1, 0)
+    below = jnp.where(place.z > 0, 1, 0)
+    pl.semaphore_wait(barrier, 3 + above + below)
+
+
+def remote(src, dst, send, recv, target):
+    return pltpu.make_async_remote_copy(
+        src_ref=src,
+        dst_ref=dst,
+        send_sem=send,
+        recv_sem=recv,
+        device_id=target,
+        device_id_type=MESH,
+    )
+
+
+def gather(place, view, parts, shared, sems):
+    send_z, send_y, send_c, send_x, recv = sems
+    nz = place.nz
+    z, y, c = place.z, place.y, place.c
+    me = (place.h, place.e)
+    shared_slot = {}
+
+    def each(fn):
+        for index, part in enumerate(parts):
+            fn(index, part)
+
+    def copy(b, part, send, target):
+        return remote(view(b, part), view(b, part), send, recv.at[b, part], target)
+
+    def arrived(b, part):
+        copy(b, part, send_c.at[0, 0, 0], me).wait_recv()
+
+    def to_core(b, index, part, slot):
+        copy(b, part, send_c.at[slot, b // 4, (b // 2) % 2], place.core()).start()
+
+    def to_head(b, index, part):
+        if index in shared:
+            copy(b, part, send_x.at[b // 4, (b // 2) % 2], place.other_head()).start()
+
+    def to_y(zz, index, part):
+        copy(place.at(zz, y, c), part, send_y.at[index, zz], place.across()).start()
+
+    def to_z(sign, zz, index, part):
+        copy(place.at(zz, y, c), part, send_z.at[index, (sign + 1) // 2, zz], place.along(sign)).start()
+
+    n = len(parts)
+    other = [None] * n
+    for index in shared:
+        other[index] = parts[index] + 1 - 2 * place.h
+
+    for index, part in enumerate(parts):
+        for sign in (-1, 1):
+
+            @pl.when(place.inside(z + sign))
+            def _():
+                to_z(sign, z, index, part)
+
+        to_y(z, index, part)
+        to_head(place.e, index, part)
+        to_core(place.e, index, part, index)
+
+    def from_z(d):
+        for index, part in enumerate(parts):
+            for sign in (-1, 1):
+                zz = z - sign * d
+
+                @pl.when(place.inside(zz))
+                def _():
+                    b = place.at(zz, y, c)
+                    arrived(b, part)
+
+                    @pl.when(place.inside(z + sign))
+                    def _():
+                        to_z(sign, zz, index, part)
+
+                    to_y(zz, index, part)
+                    to_head(b, index, part)
+                    to_core(b, index, part, index)
+
+    def at_distance(d, fn):
+        if d == 0:
+            fn(z)
+            return
+        for sign in (-1, 1):
+            zz = z - sign * d
+
+            @pl.when(place.inside(zz))
+            def _():
+                fn(zz)
+
+    def from_y(d):
+        for index, part in enumerate(parts):
+
+            def one(zz):
+                b = place.at(zz, 1 - y, c)
+                arrived(b, part)
+                to_head(b, index, part)
+                to_core(b, index, part, index)
+
+            at_distance(d, one)
+
+    def from_head(d, yy):
+        for k, index in enumerate(sorted(shared)):
+
+            def one(zz):
+                b = place.at(zz, yy, c)
+                arrived(b, other[index])
+                to_core(b, index, other[index], n + k)
+
+            at_distance(d, one)
+
+    for d in range(1, nz):
+        from_z(d)
+        from_y(d - 1)
+        from_head(d - 1, y)
+        if d > 1:
+            from_head(d - 2, 1 - y)
+    from_y(nz - 1)
+    from_head(nz - 1, y)
+    if nz > 1:
+        from_head(nz - 2, 1 - y)
+    from_head(nz - 1, 1 - y)
+
+    for zz in range(nz):
+        for yy in range(2):
+            b = place.at(zz, yy, 1 - c)
+            for part in parts:
+                arrived(b, part)
+            for index in sorted(shared):
+                arrived(b, other[index])
+
+    def settle():
+        for index, part in enumerate(parts):
+            for zz in range(nz):
+                for sign in (-1, 1):
+                    @pl.when(place.inside(z + sign) & ((z - zz) * sign >= 0))
+                    def _():
+                        copy(
+                            place.at(zz, y, c),
+                            part,
+                            send_z.at[index, (sign + 1) // 2, zz],
+                            me,
+                        ).wait_send()
+
+                copy(place.at(zz, y, c), part, send_y.at[index, zz], me).wait_send()
+                for yy in range(2):
+                    b = place.at(zz, yy, c)
+                    if index in shared:
+                        copy(b, part, send_x.at[zz, yy], me).wait_send()
+                    copy(b, part, send_c.at[index, zz, yy], me).wait_send()
+        for k, index in enumerate(sorted(shared)):
+            for zz in range(nz):
+                for yy in range(2):
+                    b = place.at(zz, yy, c)
+                    copy(b, other[index], send_c.at[n + k, zz, yy], me).wait_send()
+
+    return settle
+
+
+def layer(
+    nz,
+    plain_rows,
+    att_ref,
+    residual_ref,
+    gain_ref,
+    weight_ref,
+    w_output,
+    w_gate,
+    w_up,
+    w_down,
+    out_ref,
+    att,
+    wo,
+    wg,
+    wu,
+    wd,
+    mixed,
+    mixed_low,
+    mixed_got,
+    hidden,
+    gate_acc,
+    up_acc,
+    act,
+    partial,
+    core_got,
+    pair,
+    across_low,
+    across_got,
+    chain_low,
+    chain_got,
+    head_low,
+    head_got,
+    col_low,
+    col_got,
+    load_sem,
+    a_z,
+    a_y,
+    a_c,
+    a_x,
+    a_recv,
+    m_send,
+    m_recv,
+    h_z,
+    h_y,
+    h_c,
+    h_x,
+    h_recv,
+    rc_send,
+    rc_recv,
+    ry_send,
+    ry_recv,
+    rz_send,
+    rz_recv,
+    rx_send,
+    rx_recv,
+    rk_send,
+    rk_recv,
+):
+    place = Place(nz)
+    h, e, z, y, c = place.h, place.e, place.z, place.y, place.c
+    rows_dev, inner = att_ref.shape
+    rows, width = residual_ref.shape
+    half = rows // 2
+    quarter = rows // 4
+    blocks = nz * 4
+    me = (h, e)
+    f32, bf16 = jnp.float32, jnp.bfloat16
+
+    own = pltpu.make_async_copy(
+        att_ref, att.at[pl.ds(pl.multiple_of(e * rows_dev, rows_dev), rows_dev), :], load_sem.at[4]
+    )
+    own.start()
+    loads = [
+        pltpu.make_async_copy(src, dst, load_sem.at[i])
+        for i, (src, dst) in enumerate(((w_output, wo), (w_gate, wg), (w_up, wu), (w_down, wd)))
+    ]
+    for load in loads:
+        load.start()
+    greet(place)
+    own.wait()
+
+    def att_view(b, part):
+        return att.at[
+            pl.ds(pl.multiple_of(b * rows_dev, rows_dev), rows_dev),
+            pl.ds(part * (inner // 2), inner // 2),
+        ]
+
+    settle_att = gather(place, att_view, [0, 1], (), (a_z, a_y, a_c, a_x, a_recv))
+
+    loads[0].wait()
+    mixed[...] = jnp.zeros_like(mixed)
+    step = inner // 8
+
+    def project(k, carry):
+        at = pl.multiple_of(k * step, step)
+        mixed[...] += lax.dot_general(
+            att[:, pl.ds(at, step)],
+            wo[:, pl.ds(at, step)],
+            (((1,), (1,)), ((), ())),
+            preferred_element_type=f32,
+        )
+        return carry
+
+    lax.fori_loop(0, 8, project, 0)
+    mixed_low[...] = mixed[...].astype(bf16)
+
+    split_rows = (rows - plain_rows) // 2
+
+    def part_rows(part):
+        if isinstance(part, int) and part == 0:
+            return pl.ds(0, plain_rows)
+        return pl.ds(pl.multiple_of(plain_rows + (part - 1) * split_rows, 16), split_rows)
+
+    exchange = []
+    for index, (there, here) in enumerate(((0, 0), (2 - h, 1 + h))):
+        out = remote(
+            mixed_low.at[part_rows(there)],
+            mixed_got.at[part_rows(there)],
+            m_send.at[index],
+            m_recv.at[index],
+            place.other_head(),
+        )
+        out.start()
+        exchange.append((out, here))
+    for index, (out, here) in enumerate(exchange):
+        remote(
+            mixed_low.at[part_rows(here)],
+            mixed_got.at[part_rows(here)],
+            m_send.at[index],
+            m_recv.at[index],
+            me,
+        ).wait_recv()
+        at = part_rows(here)
+        total = mixed_low[at, :].astype(f32) + mixed_got[at, :].astype(f32)
+        hidden[e, at, :] = (residual_ref[at, :].astype(f32) + total).astype(bf16)
+
+    def hidden_view(b, part):
+        return hidden.at[b, part_rows(part)]
+
+    settle_hidden = gather(place, hidden_view, [0, 1 + h], (1,), (h_z, h_y, h_c, h_x, h_recv))
+
+    def square(b, total):
+        values = hidden[b].astype(f32)
+        return total + jnp.sum(values * values, axis=1, keepdims=True)
+
+    squares = lax.fori_loop(0, blocks, square, jnp.zeros((rows, 1), f32))
+    inverse = lax.rsqrt(squares * (1.0 / (blocks * width)) + 1e-06)
+    loads[1].wait()
+    loads[2].wait()
+    gate_acc[...] = jnp.zeros_like(gate_acc)
+    up_acc[...] = jnp.zeros_like(up_acc)
+
+    def raise_up(b, carry):
+        normed = (hidden[b].astype(f32) * inverse * gain_ref[b].astype(f32)).astype(bf16)
+        at = pl.ds(pl.multiple_of(b * width, 64), width)
+        gate_acc[...] += jnp.dot(normed, wg[at, :], preferred_element_type=f32)
+        up_acc[...] += jnp.dot(normed, wu[at, :], preferred_element_type=f32)
+        return carry
+
+    lax.fori_loop(0, blocks, raise_up, 0)
+    gate = gate_acc[...]
+    act[...] = (jax.nn.silu(gate) * up_acc[...] * weight_ref[...]).astype(bf16)
+    loads[3].wait()
+
+    pair_width = 2 * width
+
+    def down(zz, yy):
+        q = zz * 2 + yy
+        at = pl.ds(pl.multiple_of(q * pair_width, 128), pair_width)
+        value = jnp.dot(act[...], wd[:, at], preferred_element_type=f32)
+        partial[q] = value.astype(bf16).reshape(partial.shape[1:])
+        remote(
+            partial.at[q, :, 1 - c], core_got.at[q], rc_send.at[q], rc_recv.at[q], place.core()
+        ).start()
+
+    def join(zz, yy):
+        q = zz * 2 + yy
+        remote(
+            partial.at[q, :, 1 - c], core_got.at[q], rc_send.at[q], rc_recv.at[q], me
+        ).wait()
+        return partial[q, :, c].astype(f32) + core_got[q].astype(f32)
+
+    def cross(zz):
+        across_low[zz] = join(zz, 1 - y).astype(bf16)
+        remote(
+            across_low.at[zz], across_got.at[zz], ry_send.at[zz], ry_recv.at[zz], place.across()
+        ).start()
+
+    def far_to_near(fn):
+        for d in range(nz - 1, 0, -1):
+            for sign in (-1, 1):
+                zz = z + sign * d
+
+                @pl.when(place.inside(zz))
+                def _():
+                    fn(zz, sign)
+
+        fn(z, 0)
+
+    far_to_near(lambda zz, sign: down(zz, 1 - y))
+
+    def second(zz, sign):
+        cross(zz)
+        down(zz, y)
+
+    far_to_near(second)
+
+    def chain_copy(sign, zz, target):
+        way = (sign + 1) // 2
+        return remote(
+            chain_low.at[way, zz],
+            chain_got.at[way, zz],
+            rz_send.at[way, zz],
+            rz_recv.at[way, zz],
+            target,
+        )
+
+    def merge(zz, sign):
+        pair[...] = join(zz, y)
+        remote(
+            across_low.at[zz], across_got.at[zz], ry_send.at[zz], ry_recv.at[zz], me
+        ).wait()
+        pair[...] += across_got[zz].astype(f32)
+        for way in (-1, 1) if sign == 0 else (sign,):
+
+            @pl.when(place.inside(z - way))
+            def _():
+                chain_copy(way, zz, me).wait_recv()
+                pair[...] += chain_got[(way + 1) // 2, zz].astype(f32)
+
+        if sign != 0:
+            chain_low[(sign + 1) // 2, zz] = pair[...].astype(bf16)
+            chain_copy(sign, zz, place.along(sign)).start()
+
+    far_to_near(merge)
+
+    head_low[...] = pair[1 - h].astype(bf16)
+    over = remote(head_low, head_got, rx_send, rx_recv, place.other_head())
+    over.start()
+    over.wait()
+    total = pair[h] + head_got[...].astype(f32)
+    left, right = total[:, :width], total[:, width:]
+    mine = jnp.where(c == 0, left, right)
+    col_low[...] = jnp.where(c == 0, right, left).astype(bf16)
+    swap = remote(col_low, col_got, rk_send, rk_recv, place.core())
+    swap.start()
+    low = pl.multiple_of(c * quarter, quarter)
+    start = pl.multiple_of(h * half + low, quarter)
+    out_ref[pl.ds(low, quarter), :] = (
+        hidden[e, pl.ds(start, quarter), :].astype(f32) + mine
+    ).astype(out_ref.dtype)
+    low = pl.multiple_of((1 - c) * quarter, quarter)
+    start = pl.multiple_of(h * half + low, quarter)
+    swap.wait()
+    out_ref[pl.ds(low, quarter), :] = (
+        hidden[e, pl.ds(start, quarter), :].astype(f32) + col_got[...].astype(f32)
+    ).astype(out_ref.dtype)
+
+    settle_att()
+    for out, _ in exchange:
+        out.wait_send()
+    settle_hidden()
+    for zz in range(nz):
+        for sign in (-1, 1):
+
+            @pl.when((zz - z) * sign > 0)
+            def _():
+                chain_copy(sign, zz, me).wait_send()
+
+
+def fused_layer(nz, attention, w_output, residual, gain, weight, w_gate, w_up, w_down):
+    rows_dev, inner = attention.shape
+    rows, width = residual.shape
+    d_model, hidden_units = w_gate.shape
+    blocks = nz * 4
+    quarter = rows // 4
+    pair_width = 2 * width
+    bf16, f32 = jnp.bfloat16, jnp.float32
+    plain_rows = rows * 3 // 8
+    dma = pltpu.SemaphoreType.DMA
+    vmem = pl.BlockSpec(memory_space=pltpu.VMEM)
+    hbm = pl.BlockSpec(memory_space=pl.ANY)
+    block = (2, quarter, pair_width)
+    return pl.pallas_call(
+        functools.partial(layer, nz, plain_rows),
+        out_shape=jax.ShapeDtypeStruct((rows // 2, width), bf16),
+        in_specs=[vmem, vmem, vmem, vmem, hbm, hbm, hbm, hbm],
+        out_specs=vmem,
+        scratch_shapes=[
+            pltpu.VMEM((rows, inner), bf16),
+            pltpu.VMEM(w_output.shape, bf16),
+            pltpu.VMEM(w_gate.shape, bf16),
+            pltpu.VMEM(w_up.shape, bf16),
+            pltpu.VMEM(w_down.shape, bf16),
+            pltpu.VMEM((rows, width), f32),
+            pltpu.VMEM((rows, width), bf16),
+            pltpu.VMEM((rows, width), bf16),
+            pltpu.VMEM((blocks, rows, width), bf16),
+            pltpu.VMEM((rows, hidden_units), f32),
+            pltpu.VMEM((rows, hidden_units), f32),
+            pltpu.VMEM((rows, hidden_units), bf16),
+            pltpu.VMEM((nz * 2, 2, 2, quarter, pair_width), bf16),
+            pltpu.VMEM((nz * 2,) + block, bf16),
+            pltpu.VMEM(block, f32),
+            pltpu.VMEM((nz,) + block, bf16),
+            pltpu.VMEM((nz,) + block, bf16),
+            pltpu.VMEM((2, nz) + block, bf16),
+            pltpu.VMEM((2, nz) + block, bf16),
+            pltpu.VMEM(block[1:], bf16),
+            pltpu.VMEM(block[1:], bf16),
+            pltpu.VMEM((quarter, width), bf16),
+            pltpu.VMEM((quarter, width), bf16),
+            dma((5,)),
+            dma((2, 2, nz)),
+            dma((2, nz)),
+            dma((2, nz, 2)),
+            dma((1, 1)),
+            dma((blocks, 2)),
+            dma((2,)),
+            dma((2,)),
+            dma((2, 2, nz)),
+            dma((2, nz)),
+            dma((3, nz, 2)),
+            dma((nz, 2)),
+            dma((blocks, 3)),
+            dma((nz * 2,)),
+            dma((nz * 2,)),
+            dma((nz,)),
+            dma((nz,)),
+            dma((2, nz)),
+            dma((2, nz)),
+            dma,
+            dma,
+            dma,
+            dma,
+        ],
+        compiler_params=pltpu.CompilerParams(
+            collective_id=0, has_side_effects=True, vmem_limit_bytes=62 * 2**20
+        ),
+        name="fused_layer",
+    )(attention, residual, gain, weight, w_output, w_gate, w_up, w_down)
 
 
 def per_device(
@@ -98,21 +647,38 @@
         axis=0,
         mode="clip",
     )
-    arrived = lax.all_gather(arrived_share, "head", axis=1, tiled=True)
+    if n_head == 2:
+        other = lax.ppermute(arrived_share, "head", [(0, 1), (1, 0)])
+        first = jnp.where(head_index == 0, arrived_share, other)
+        last = jnp.where(head_index == 0, other, arrived_share)
+        arrived = jnp.concatenate([first, last], axis=1)
+    else:
+        arrived = lax.all_gather(arrived_share, "head", axis=1, tiled=True)
     resident_att = attend(queries[:req_count], resident_cache, resident_len, value_up)
     arrived_att = attend(queries[req_count:], arrived, new_len[chosen], value_up)
     attention = jnp.concatenate([resident_att, arrived_att], axis=0)
+
+    if n_head == 2 and n_expert % 4 == 0 and local_experts == 1:
+        mine = expert_ids == owner_index
+        weight = jnp.sum(jnp.where(mine, expert_gates, 0.0), axis=1, keepdims=True)
+        return fused_layer(
+            n_expert // 4,
+            attention,
+            w_output.T,
+            residual,
+            norm_gain.reshape(n_expert, 1, -1),
+            weight,
+            w_gate[0],
+            w_up[0],
+            w_down[0],
+        )
+
     mixed = jnp.dot(
         lax.all_gather(attention, "expert", axis=0, tiled=True),
         w_output,
         preferred_element_type=jnp.float32,
     ).T
-    swap = [(0, 1), (1, 0)]
-    if n_head == 2:
-        mixed = mixed.astype(jnp.bfloat16)
-        summed = mixed.astype(jnp.float32) + lax.ppermute(mixed, "head", swap).astype(jnp.float32)
-    else:
-        summed = lax.psum(mixed, "head")
+    summed = lax.psum(mixed, "head")
     hidden = (residual.T.astype(jnp.float32) + summed).astype(jnp.bfloat16)
     hidden_block = lax.dynamic_slice_in_dim(hidden, head_index * block_rows, block_rows, axis=1)
 
@@ -132,15 +698,9 @@
     routed = lax.psum_scatter(
         partial.astype(jnp.bfloat16), "expert", scatter_dimension=0, tiled=True
     )
-    if n_head == 2:
-        kept = lax.dynamic_slice_in_dim(routed, head_index * block_rows, block_rows, axis=1)
-        sent = lax.dynamic_slice_in_dim(routed, (1 - head_index) * block_rows, block_rows, axis=1)
-        got = lax.ppermute(sent, "head", swap)
-        routed_block = kept.astype(jnp.float32) + got.astype(jnp.float32)
-    else:
-        routed_block = lax.psum_scatter(
-            routed, "head", scatter_dimension=1, tiled=True
-        ).astype(jnp.float32)
+    routed_block = lax.psum_scatter(routed, "head", scatter_dimension=1, tiled=True).astype(
+        jnp.float32
+    )
     return (hidden_block.astype(jnp.float32) + routed_block).astype(jnp.bfloat16).T
 
 

time: 291 us -> 169 us (0.58)
  waiting for transfers between devices: 193 us -> 27.4 us
  Pallas kernels: 0 us -> 106 us
  matrix products: 44.4 us -> 14.5 us
  blocking collectives: 14.8 us -> 0 us
  between operations: 13.3 us -> 0.22 us
  other arithmetic: 8.7 us -> 2.72 us
    pallas_call x0 -> x1, Pallas kernels: none -> 106 us  [fused_layer(): pl.pallas_call(functools.partial(layer, nz, plain_rows), out_shape=jax.Sh...]
    all_gather x2 -> x0, waiting for transfers between devices: 99.2 us -> none  [the longest x1 53.2 us: per_device(): lax.all_gather(attention, 'expert', axis=0, tiled=True)]
    reduce_scatter x1 -> x0, waiting for transfers between devices: 67.5 us -> none  [per_device(): lax.psum_scatter(partial.astype(jnp.bfloat16), 'expert', scatter_dimensio...]
    dot_general x3 -> x0, matrix products: 28 us -> none  [the longest x1 13.2 us: per_device(): jnp.einsum('fd,fr->dr', w_down[e], act, preferred_element_type=jnp.float32)]
    all_gather x1 -> x0, blocking collectives: 14.8 us -> none  [per_device(): arrived = lax.all_gather(arrived_share, 'head', axis=1, tiled=True)]
    all_to_all x1, waiting for transfers between devices: 16.5 us -> 20 us  [per_device(): lax.all_to_all(outgoing, 'expert', split_axis=0, concat_axis=0, tiled=True)]
    reduce_sum x2 -> x1, other arithmetic: 3.03 us -> 0.02 us  [per_device(): weight = jnp.sum(jnp.where(mine, expert_gates, 0.0), axis=1, keepdims=True)]
    ppermute x2 -> x1, waiting for transfers between devices: 9.63 us -> 7.36 us  [per_device(): other = lax.ppermute(arrived_share, 'head', [(0, 1), (1, 0)])]
  transfers between devices with their start and end apart: 6 -> 2, of which waited for: 6 -> 2; matrix products, arithmetic and copies ran while one was open for 4% -> 7% of each run, Pallas kernels for 0% -> 0%
where the time goes in v1:
time: 169 us; the launch traced here: 168 us
  Pallas kernels  106 us (63%)
  waiting for transfers between devices  27.4 us (16%)
  matrix products  14.5 us (9%)
  starting transfers between devices  9.11 us (5%)
  local copies, waits for them, and re-layouts  8.26 us (5%)
  other arithmetic  2.72 us (2%)
    pallas_call x1, Pallas kernels, fused_layer(): pl.pallas_call(functools.partial(layer, nz, plain_rows), out_shape=jax.Sh...  106 us
    all_to_all x1, waiting for transfers between devices, per_device(): lax.all_to_all(outgoing, 'expert', split_axis=0, concat_axis=0, tiled=True)  20 us
    dot_general x2, matrix products, attend(): jnp.einsum('rhc,hcv->rhv', latent, value_up, preferred_element_type=jnp.f...  10.1 us
    all_to_all x1, starting transfers between devices, per_device(): lax.all_to_all(outgoing, 'expert', split_axis=0, concat_axis=0, tiled=True)  7.56 us
    ppermute x1, waiting for transfers between devices, per_device(): other = lax.ppermute(arrived_share, 'head', [(0, 1), (1, 0)])  7.36 us
  transfers between devices with their start and end apart: 2, of which 2 were waited for; matrix products, arithmetic and copies ran while one was open for 7% of the time, Pallas kernels for 0%

profile of v1, /device:TPU:0, one launch (start us, length us, event | category | flops | bytes accessed | tf_op | source)
XLA Modules:
  0.0 168.3 jit_solution(15081235316156211809)
XLA Ops:
  0.0 0.8 dynamic_slice.7
  0.8 0.2 convert_reduce_fusion.2
  1.0 0.8 multiply_add_fusion
  2.0 1.8 %gather_fusion.1 = bf16[32,32,576]{2,1,0:T(8,128)(2,1)} fusion(bf16[12,32,576]{2,1,0:T(8,128)(2,1)S(1)} %constant_dynamic-slice_fusion, s32[1024]{0:T(1024)S(1)} %pad_clamp_fusion.1), kind=kCustom, calls=%fused_computation.1 | custom fusion | bytes 2359424 | tf_op jit(solution)/shard_map/jit(_take)/gather | solution.py:627
  3.8 7.6 %all-to-all-start = ((bf16[16,2,32,576]{3,2,1,0:T(8,128)(2,1)}), bf16[16,2,32,576]{3,2,1,0:T(8,128)(2,1)S(1)}, u32[]{:S(2)}, u32[]{:S(2)}) async-start(bf16[16,2,32,576]{3,2,1,0:T(8,128)(2,1)} %bitcast.4), calls=%async_computation | async-start | bytes 2621440 | tf_op jit(solution)/shard_map/all_to_all | solution.py:630
  11.4 0.8 copy.31.weight_ref
  12.2 0.9 copy.29.residual_ref
  13.0 0.7 reshape.119.gain_ref
  14.0 0.2 convert_reduce_fusion.1
  14.2 0.7 gather_fusion
  14.9 1.7 %fusion.9 = f32[4,64,256]{2,1,0:T(8,128)S(1)} fusion(bf16[16,64,576]{2,1,0:T(8,128)(2,1)} %param.15, bf16[4,256,576]{1,2,0:T(8,128)(2,1)} %param.16, s32[4]{0:T(128)S(1)} %copy-done.9), kind=kOutput, calls=%fused_computation.17 | convolution fusion | flops 75694080 | bytes 2621456 | tf_op jit(solution)/shard_map/rhc,rtc->rht/dot_general | solution.py:19
  16.6 0.2 fusion.35
  16.8 1.8 %convolution_convert_fusion.2 = bf16[4,64,512]{2,1,0:T(8,128)(2,1)S(1)} fusion(bf16[4,256,576]{1,2,0:T(8,128)(2,1)} %param.16, f32[4,64]{1,0:T(4,128)S(1)} %fusion.35, f32[4,64,256]{2,1,0:T(8,128)S(1)} %fusion.9), kind=kOutput, calls=%fused_computation.12 | convolution fusion | flops 67437056 | bytes 1837056 | tf_op jit(solution)/shard_map/rht,rtc->rhc/dot_general | solution.py:27
  18.6 20.0 %all-to-all-done = bf16[16,2,32,576]{3,2,1,0:T(8,128)(2,1)S(1)} async-done(((bf16[16,2,32,576]{3,2,1,0:T(8,128)(2,1)}), bf16[16,2,32,576]{3,2,1,0:T(8,128)(2,1)S(1)}, u32[]{:S(2)}, u32[]{:S(2)}) %all-to-all-start) | async-done | bytes 1179680 | tf_op jit(solution)/shard_map/all_to_all | solution.py:630
  38.6 0.6 gather_fusion.2
  39.2 1.6 collective-permute-start
  40.8 5.2 %fusion.10 = bf16[4,8192]{1,0:T(4,128)(2,1)} fusion(bf16[64,512,128]{2,1,0:T(8,128)(2,1)} %param.21, bf16[4,64,512]{2,1,0:T(8,128)(2,1)S(1)} %convolution_convert_fusion.2), kind=kOutput, calls=%fused_computation.19 | convolution fusion | flops 33587200 | bytes 8716288 | tf_op jit(solution)/shard_map/rhc,hcv->rhv/dot_general | solution.py:30
  46.0 7.4 %collective-permute-done = bf16[12,32,576]{2,1,0:T(8,128)(2,1)S(1)} collective-permute-done((bf16[12,32,576]{2,1,0:T(8,128)(2,1)S(1)}, bf16[12,32,576]{2,1,0:T(8,128)(2,1)S(1)}, u32[]{:S(2)}, u32[]{:S(2)}) %collective-permute-start) | collective-permute-done | bytes 442400 | tf_op jit(solution)/shard_map/ppermute | solution.py:651
  53.5 0.5 fusion.6
  54.1 0.4 convolution_convert_fusion
  54.6 4.9 %fusion.8 = bf16[12,64,128]{2,0,1:T(8,128)(2,1)S(1)} fusion(bf16[64,512,128]{2,1,0:T(8,128)(2,1)} %param.21, bf16[12,64,512]{2,1,0:T(8,128)(2,1)S(1)} %convolution_convert_fusion), kind=kOutput, calls=%fused_computation.15 | convolution fusion | flops 100761600 | bytes 9371648 | tf_op jit(solution)/shard_map/rhc,hcv->rhv/dot_general | solution.py:30
  59.7 0.8 pad_maximum_fusion.att_ref
  60.5 106.1 %fused_layer.1 = bf16[128,448]{1,0:T(8,128)(2,1)} custom-call(bf16[16,8192]{1,0:T(8,128)(2,1)} %pad_maximum_fusion.att_ref, bf16[256,448]{1,0:T(8,128)(2,1)} %copy.29.residual_ref, bf16[16,1,448]{2,1,0:T(2,128)(2,1)} %reshape.119.gain_ref, f32[256,1]{1,0:T(8,128)} %copy.31.weight_ref, bf16[448,8192]{1,0:T(8,128)(2,1)} %bitcast.49, ...), custom_call_target="tpu_custom_call" | custom-call | tf_op jit(solution)/shard_map/fused_layer/pallas_call | solution.py:527
  166.6 1.7 copy.32
  (36 shorter events, 1.0 us)
Async XLA Ops:
  0.0 1.9 %copy-start = (bf16[12,64,576]{2,1,0:T(8,128)(2,1)S(1)}, bf16[12,64,576]{2,1,0:T(8,128)(2,1)}, u32[]{:S(2)}) copy-start(bf16[12,64,576]{2,1,0:T(8,128)(2,1)} %param.18) | copy-start | bytes 2654212
  3.7 7.6 %copy-start.5 = (f32[256,8]{0,1:T(8,128)S(1)}, f32[256,8]{0,1:T(8,128)}, u32[]{:S(2)}) copy-start(f32[256,8]{0,1:T(8,128)} %param.25) | copy-start | bytes 24580
  3.7 7.6 %copy-start.6 = (s32[256,8]{0,1:T(8,128)S(1)}, s32[256,8]{0,1:T(8,128)}, u32[]{:S(2)}) copy-start(s32[256,8]{0,1:T(8,128)} %param.24) | copy-start | bytes 24580
  3.7 8.4 %copy-start.3 = (bf16[256,448]{0,1:T(8,128)(2,1)S(1)}, bf16[256,448]{0,1:T(8,128)(2,1)}, u32[]{:S(2)}) copy-start(bf16[256,448]{0,1:T(8,128)(2,1)} %param.23) | copy-start | bytes 688132
  3.7 9.3 %copy-start.4 = (bf16[7168]{0:T(1024)(128)(2,1)S(1)}, bf16[7168]{0:T(1024)(128)(2,1)}, u32[]{:S(2)}) copy-start(bf16[7168]{0:T(1024)(128)(2,1)} %param.26) | copy-start | bytes 43012
  3.7 10.0 %copy-start.7 = (s32[192]{0:T(256)S(1)}, s32[192]{0:T(256)}, u32[]{:S(2)}) copy-start(s32[192]{0:T(256)} %param.20) | copy-start | bytes 2308
  3.7 10.5 %copy-start.1 = (s32[192]{0:T(256)S(1)}, s32[192]{0:T(256)}, u32[]{:S(2)}) copy-start(s32[192]{0:T(256)} %param.19) | copy-start | bytes 2308
  3.7 11.1 %copy-start.9 = (s32[4]{0:T(128)S(1)}, s32[4]{0:T(128)}, u32[]{:S(2)}) copy-start(s32[4]{0:T(128)} %param.17) | copy-start | bytes 52
  3.8 34.8 %all-to-all-start = ((bf16[16,2,32,576]{3,2,1,0:T(8,128)(2,1)}), bf16[16,2,32,576]{3,2,1,0:T(8,128)(2,1)S(1)}, u32[]{:S(2)}, u32[]{:S(2)}) async-start(bf16[16,2,32,576]{3,2,1,0:T(8,128)(2,1)} %bitcast.4), calls=%async_computation | async-start | bytes 2621440 | tf_op jit(solution)/shard_map/all_to_all | solution.py:630
  39.2 14.2 %collective-permute-start = (bf16[12,32,576]{2,1,0:T(8,128)(2,1)S(1)}, bf16[12,32,576]{2,1,0:T(8,128)(2,1)S(1)}, u32[]{:S(2)}, u32[]{:S(2)}) collective-permute-start(bf16[12,32,576]{2,1,0:T(8,128)(2,1)S(1)} %gather_fusion.2), channel_id=1, source_target_pairs={{0,16},{16,0},{1,17},{17,1},{2,18},{18,2},{3,19},{19,3},{4,20},{20... | collective-permute-start | bytes 1327112 | tf_op jit(solution)/shard_map/ppermute | solution.py:651
  46.0 7.5 %copy-start.8 = (bf16[16,64,576]{2,1,0:T(8,128)(2,1)S(1)}, bf16[16,64,576]{2,1,0:T(8,128)(2,1)}, u32[]{:S(2)}) copy-start(bf16[16,64,576]{2,1,0:T(8,128)(2,1)} %param.15) | copy-start | bytes 3538948
  54.6 5.2 %copy-start.2 = (bf16[4,8192]{1,0:T(4,128)(2,1)S(1)}, bf16[4,8192]{1,0:T(4,128)(2,1)}, u32[]{:S(2)}) copy-start(bf16[4,8192]{1,0:T(4,128)(2,1)} %fusion.10) | copy-start | bytes 196612

commit v2 on v1

--- a/solution.py
+++ b/solution.py
@@ -27,6 +27,10 @@
     latent = jnp.einsum(
         "rht,rtc->rhc", weights, caches[:, :, :latent_width], preferred_element_type=jnp.float32
     ).astype(jnp.bfloat16)
+    return raise_values(latent, value_up)
+
+
+def raise_values(latent, value_up):
     values = jnp.einsum(
         "rhc,hcv->rhv", latent, value_up, preferred_element_type=jnp.float32
     ).astype(jnp.bfloat16)
@@ -243,10 +247,12 @@
 def layer(
     nz,
     plain_rows,
+    n_early,
     att_ref,
     residual_ref,
     gain_ref,
-    weight_ref,
+    ids_ref,
+    gates_ref,
     w_output,
     w_gate,
     w_up,
@@ -257,6 +263,7 @@
     wg,
     wu,
     wd,
+    base,
     mixed,
     mixed_low,
     mixed_got,
@@ -266,6 +273,9 @@
     act,
     partial,
     core_got,
+    joined,
+    early_low,
+    early_got,
     pair,
     across_low,
     across_got,
@@ -290,6 +300,8 @@
     h_recv,
     rc_send,
     rc_recv,
+    re_send,
+    re_recv,
     ry_send,
     ry_recv,
     rz_send,
@@ -301,26 +313,25 @@
 ):
     place = Place(nz)
     h, e, z, y, c = place.h, place.e, place.z, place.y, place.c
-    rows_dev, inner = att_ref.shape
-    rows, width = residual_ref.shape
+    heads, rows_dev, value_width = att_ref.shape
+    inner = heads * value_width
+    width, rows = residual_ref.shape
     half = rows // 2
     quarter = rows // 4
     blocks = nz * 4
     me = (h, e)
     f32, bf16 = jnp.float32, jnp.bfloat16
 
-    own = pltpu.make_async_copy(
-        att_ref, att.at[pl.ds(pl.multiple_of(e * rows_dev, rows_dev), rows_dev), :], load_sem.at[4]
-    )
-    own.start()
     loads = [
         pltpu.make_async_copy(src, dst, load_sem.at[i])
         for i, (src, dst) in enumerate(((w_output, wo), (w_gate, wg), (w_up, wu), (w_down, wd)))
     ]
     for load in loads:
         load.start()
+    own_rows = pl.ds(pl.multiple_of(e * rows_dev, rows_dev), rows_dev)
+    for k in range(heads):
+        att[own_rows, k * value_width : (k + 1) * value_width] = att_ref[k]
     greet(place)
-    own.wait()
 
     def att_view(b, part):
         return att.at[
@@ -330,6 +341,9 @@
 
     settle_att = gather(place, att_view, [0, 1], (), (a_z, a_y, a_c, a_x, a_recv))
 
+    base[...] = residual_ref[...].astype(f32).T
+    mine = jnp.where(ids_ref[...] == e, gates_ref[...], 0.0)
+    weight = jnp.sum(mine.T, axis=1, keepdims=True)
     loads[0].wait()
     mixed[...] = jnp.zeros_like(mixed)
     step = inner // 8
@@ -375,7 +389,7 @@
         ).wait_recv()
         at = part_rows(here)
         total = mixed_low[at, :].astype(f32) + mixed_got[at, :].astype(f32)
-        hidden[e, at, :] = (residual_ref[at, :].astype(f32) + total).astype(bf16)
+        hidden[e, at, :] = (base[at, :] + total).astype(bf16)
 
     def hidden_view(b, part):
         return hidden.at[b, part_rows(part)]
@@ -402,86 +416,128 @@
 
     lax.fori_loop(0, blocks, raise_up, 0)
     gate = gate_acc[...]
-    act[...] = (jax.nn.silu(gate) * up_acc[...] * weight_ref[...]).astype(bf16)
+    act[...] = (jax.nn.silu(gate) * up_acc[...] * weight).astype(bf16)
     loads[3].wait()
 
     pair_width = 2 * width
+    early, late = pl.ds(0, n_early), pl.ds(n_early, joined.shape[1] - n_early)
+    n_late = quarter - n_early
 
     def down(zz, yy):
         q = zz * 2 + yy
         at = pl.ds(pl.multiple_of(q * pair_width, 128), pair_width)
         value = jnp.dot(act[...], wd[:, at], preferred_element_type=f32)
         partial[q] = value.astype(bf16).reshape(partial.shape[1:])
-        remote(
-            partial.at[q, :, 1 - c], core_got.at[q], rc_send.at[q], rc_recv.at[q], place.core()
-        ).start()
-
-    def join(zz, yy):
-        q = zz * 2 + yy
-        remote(
-            partial.at[q, :, 1 - c], core_got.at[q], rc_send.at[q], rc_recv.at[q], me
-        ).wait()
-        return partial[q, :, c].astype(f32) + core_got[q].astype(f32)
-
-    def cross(zz):
-        across_low[zz] = join(zz, 1 - y).astype(bf16)
-        remote(
-            across_low.at[zz], across_got.at[zz], ry_send.at[zz], ry_recv.at[zz], place.across()
-        ).start()
-
-    def far_to_near(fn):
-        for d in range(nz - 1, 0, -1):
-            for sign in (-1, 1):
-                zz = z + sign * d
-
-                @pl.when(place.inside(zz))
+        core_copy(q, place.core()).start()
+
+    def core_copy(q, target):
+        return remote(
+            partial.at[q, :, 1 - c], core_got.at[q], rc_send.at[q], rc_recv.at[q], target
+        )
+
+    def early_copy(q, target):
+        return remote(early_low.at[q], early_got.at[q], re_send.at[q], re_recv.at[q], target)
+
+    def across_copy(zz, k, target):
+        at = (early, late)[k]
+        return remote(
+            across_low.at[zz, at],
+            across_got.at[zz, at],
+            ry_send.at[zz, k],
+            ry_recv.at[zz, k],
+            target,
+        )
+
+    def chain_copy(sign, zz, k, target):
+        way, at = (sign + 1) // 2, (early, late)[k]
+        return remote(
+            chain_low.at[way, zz, at],
+            chain_got.at[way, zz, at],
+            rz_send.at[way, zz, k],
+            rz_recv.at[way, zz, k],
+            target,
+        )
+
+    def at_distance(d, fn):
+        if d == 0:
+            fn(z, 0)
+            return
+        for sign in (-1, 1):
+            zz = z + sign * d
+
+            @pl.when(place.inside(zz))
+            def _():
+                fn(zz, sign)
+
+    def both_down(zz, sign):
+        down(zz, 1 - y)
+        down(zz, y)
+
+    def join(zz, sign):
+        for k, yy in enumerate((1 - y, y)):
+            q = zz * 2 + yy
+            core_copy(q, me).wait()
+
+            def total(head, at):
+                return partial[q, head, c, at].astype(f32) + core_got[q, head, at].astype(f32)
+
+            early_low[q] = total(1 - h, early).astype(bf16)
+            early_copy(q, place.other_head()).start()
+            joined[q, early] = total(h, early)
+            rest = [total(head, pl.ds(n_early, n_late)) for head in range(2)]
+            if k == 0:
+                across_low[zz, late] = jnp.concatenate(rest, axis=0).astype(bf16)
+                across_copy(zz, 1, place.across()).start()
+            else:
+                joined[q, late] = jnp.concatenate(rest, axis=0)
+
+    def cross(zz, sign):
+        q = zz * 2 + 1 - y
+        early_copy(q, me).wait()
+        across_low[zz, early] = (joined[q, early] + early_got[q].astype(f32)).astype(bf16)
+        across_copy(zz, 0, place.across()).start()
+
+    def merge(zz, sign):
+        q = zz * 2 + y
+        pair[...] = joined[q]
+        for k in (1, 0):
+            at = (early, late)[k]
+            if k == 0:
+                early_copy(q, me).wait()
+                pair[at, :] += early_got[q].astype(f32)
+            across_copy(zz, k, me).wait()
+            pair[at, :] += across_got[zz, at].astype(f32)
+            for way in (-1, 1) if sign == 0 else (sign,):
+
+                @pl.when(place.inside(z - way))
                 def _():
-                    fn(zz, sign)
-
-        fn(z, 0)
-
-    far_to_near(lambda zz, sign: down(zz, 1 - y))
-
-    def second(zz, sign):
-        cross(zz)
-        down(zz, y)
-
-    far_to_near(second)
-
-    def chain_copy(sign, zz, target):
-        way = (sign + 1) // 2
-        return remote(
-            chain_low.at[way, zz],
-            chain_got.at[way, zz],
-            rz_send.at[way, zz],
-            rz_recv.at[way, zz],
-            target,
-        )
-
-    def merge(zz, sign):
-        pair[...] = join(zz, y)
-        remote(
-            across_low.at[zz], across_got.at[zz], ry_send.at[zz], ry_recv.at[zz], me
-        ).wait()
-        pair[...] += across_got[zz].astype(f32)
-        for way in (-1, 1) if sign == 0 else (sign,):
-
-            @pl.when(place.inside(z - way))
-            def _():
-                chain_copy(way, zz, me).wait_recv()
-                pair[...] += chain_got[(way + 1) // 2, zz].astype(f32)
-
-        if sign != 0:
-            chain_low[(sign + 1) // 2, zz] = pair[...].astype(bf16)
-            chain_copy(sign, zz, place.along(sign)).start()
-
-    far_to_near(merge)
-
-    head_low[...] = pair[1 - h].astype(bf16)
+                    chain_copy(way, zz, k, me).wait_recv()
+                    pair[at, :] += chain_got[(way + 1) // 2, zz, at].astype(f32)
+
+            if sign != 0:
+                chain_low[(sign + 1) // 2, zz, at] = pair[at, :].astype(bf16)
+                chain_copy(sign, zz, k, place.along(sign)).start()
+
+    for d in range(nz - 1, -1, -1):
+        at_distance(d, both_down)
+    for d in range(nz - 1, -1, -1):
+        at_distance(d, join)
+    at_distance(nz - 1, cross)
+    for d in range(nz - 1, -1, -1):
+        if d > 0:
+            at_distance(d - 1, cross)
+        at_distance(d, merge)
+
+    def late_rows(head):
+        return pl.ds(pl.multiple_of(n_early + head * n_late, 16), n_late)
+
+    head_low[...] = pair[late_rows(1 - h), :].astype(bf16)
     over = remote(head_low, head_got, rx_send, rx_recv, place.other_head())
     over.start()
     over.wait()
-    total = pair[h] + head_got[...].astype(f32)
+    total = jnp.concatenate(
+        [pair[early, :], pair[late_rows(h), :] + head_got[...].astype(f32)], axis=0
+    )
     left, right = total[:, :width], total[:, width:]
     mine = jnp.where(c == 0, left, right)
     col_low[...] = jnp.where(c == 0, right, left).astype(bf16)
@@ -508,12 +564,14 @@
 
             @pl.when((zz - z) * sign > 0)
             def _():
-                chain_copy(sign, zz, me).wait_send()
-
-
-def fused_layer(nz, attention, w_output, residual, gain, weight, w_gate, w_up, w_down):
-    rows_dev, inner = attention.shape
-    rows, width = residual.shape
+                for k in range(2):
+                    chain_copy(sign, zz, k, me).wait_send()
+
+
+def fused_layer(nz, attention, w_output, residual, gain, ids, gates, w_gate, w_up, w_down):
+    heads, rows_dev, value_width = attention.shape
+    inner = heads * value_width
+    width, rows = residual.shape
     d_model, hidden_units = w_gate.shape
     blocks = nz * 4
     quarter = rows // 4
@@ -523,11 +581,13 @@
     dma = pltpu.SemaphoreType.DMA
     vmem = pl.BlockSpec(memory_space=pltpu.VMEM)
     hbm = pl.BlockSpec(memory_space=pl.ANY)
-    block = (2, quarter, pair_width)
+    n_early = quarter * 3 // 4 // 16 * 16
+    kept = (2 * quarter - n_early, pair_width)
+    early = (nz * 2, n_early, pair_width)
     return pl.pallas_call(
-        functools.partial(layer, nz, plain_rows),
+        functools.partial(layer, nz, plain_rows, n_early),
         out_shape=jax.ShapeDtypeStruct((rows // 2, width), bf16),
-        in_specs=[vmem, vmem, vmem, vmem, hbm, hbm, hbm, hbm],
+        in_specs=[vmem, vmem, vmem, vmem, vmem, hbm, hbm, hbm, hbm],
         out_specs=vmem,
         scratch_shapes=[
             pltpu.VMEM((rows, inner), bf16),
@@ -536,6 +596,7 @@
             pltpu.VMEM(w_up.shape, bf16),
             pltpu.VMEM(w_down.shape, bf16),
             pltpu.VMEM((rows, width), f32),
+            pltpu.VMEM((rows, width), f32),
             pltpu.VMEM((rows, width), bf16),
             pltpu.VMEM((rows, width), bf16),
             pltpu.VMEM((blocks, rows, width), bf16),
@@ -543,17 +604,20 @@
             pltpu.VMEM((rows, hidden_units), f32),
             pltpu.VMEM((rows, hidden_units), bf16),
             pltpu.VMEM((nz * 2, 2, 2, quarter, pair_width), bf16),
-            pltpu.VMEM((nz * 2,) + block, bf16),
-            pltpu.VMEM(block, f32),
-            pltpu.VMEM((nz,) + block, bf16),
-            pltpu.VMEM((nz,) + block, bf16),
-            pltpu.VMEM((2, nz) + block, bf16),
-            pltpu.VMEM((2, nz) + block, bf16),
-            pltpu.VMEM(block[1:], bf16),
-            pltpu.VMEM(block[1:], bf16),
+            pltpu.VMEM((nz * 2, 2, quarter, pair_width), bf16),
+            pltpu.VMEM((nz * 2,) + kept, f32),
+            pltpu.VMEM(early, bf16),
+            pltpu.VMEM(early, bf16),
+            pltpu.VMEM(kept, f32),
+            pltpu.VMEM((nz,) + kept, bf16),
+            pltpu.VMEM((nz,) + kept, bf16),
+            pltpu.VMEM((2, nz) + kept, bf16),
+            pltpu.VMEM((2, nz) + kept, bf16),
+            pltpu.VMEM((quarter - n_early, pair_width), bf16),
+            pltpu.VMEM((quarter - n_early, pair_width), bf16),
             pltpu.VMEM((quarter, width), bf16),
             pltpu.VMEM((quarter, width), bf16),
-            dma((5,)),
+            dma((4,)),
             dma((2, 2, nz)),
             dma((2, nz)),
             dma((2, nz, 2)),
@@ -568,10 +632,12 @@
             dma((blocks, 3)),
             dma((nz * 2,)),
             dma((nz * 2,)),
-            dma((nz,)),
-            dma((nz,)),
-            dma((2, nz)),
-            dma((2, nz)),
+            dma((nz * 2,)),
+            dma((nz * 2,)),
+            dma((nz, 2)),
+            dma((nz, 2)),
+            dma((2, nz, 2)),
+            dma((2, nz, 2)),
             dma,
             dma,
             dma,
@@ -581,7 +647,201 @@
             collective_id=0, has_side_effects=True, vmem_limit_bytes=62 * 2**20
         ),
         name="fused_layer",
-    )(attention, residual, gain, weight, w_output, w_gate, w_up, w_down)
+    )(attention, residual, gain, ids, gates, w_output, w_gate, w_up, w_down)
+
+
+def weigh(scores, length):
+    inverse_root = (NOPE + ROPE) ** (-0.5)
+    inside = lax.broadcasted_iota(jnp.int32, scores.shape, 1) < length
+    scores = jnp.where(inside, scores * inverse_root, -jnp.inf)
+    raised = jnp.exp(scores - jnp.max(scores, axis=1, keepdims=True))
+    return (raised / jnp.sum(raised, axis=1, keepdims=True)).astype(jnp.bfloat16)
+
+
+def score(queries, cache):
+    return lax.dot_general(
+        queries, cache, (((1,), (1,)), ((), ())), preferred_element_type=jnp.float32
+    )
+
+
+def handoff(
+    nz,
+    most,
+    cache_hbm,
+    queries_hbm,
+    resident_hbm,
+    resident_len,
+    senders,
+    slot,
+    new_len,
+    latent_ref,
+    cache_ref,
+    outgoing_ref,
+    queries_ref,
+    resident_ref,
+    got,
+    scores,
+    load_sem,
+    own_sem,
+    send,
+    recv,
+    pass_send,
+    pass_recv,
+):
+    place = Place(nz)
+    h, e = place.h, place.e
+    count = nz * 4
+    loads = [
+        pltpu.make_async_copy(src, dst, load_sem.at[i])
+        for i, (src, dst) in enumerate(
+            ((cache_hbm, cache_ref), (queries_hbm, queries_ref), (resident_hbm, resident_ref))
+        )
+    ]
+    for load in loads:
+        load.start()
+    req_count = resident_ref.shape[0]
+    new_count = slot.shape[0]
+    width = latent_ref.shape[2]
+    me = (h, e)
+
+    half = nz // 2
+    low = (place.z // half) * half
+    order = [
+        (side, dz, dy, dc)
+        for side in (1, 0)
+        for dz in reversed(range(half))
+        for dy in (1, 0)
+        for dc in (1, 0)
+    ][: count - 1]
+
+    def partner(sign, side, dz, dy, dc):
+        base = low if side == 0 else (nz - half) - low
+        z = base + lax.rem(place.z - low + half + sign * dz, half)
+        return place.at(z, (place.y + dy) % 2, (place.c + dc) % 2)
+
+    def target(*step):
+        return partner(1, *step)
+
+    def source(*step):
+        return partner(-1, *step)
+
+    def unit(ref, b, head=None):
+        at = pl.ds(b * most, most)
+        return ref.at[at] if head is None else ref.at[at, head]
+
+    def positions(step):
+        return h if step[0] == 1 else None
+
+    def sent(index, there, target_id):
+        part = positions(order[index])
+        return remote(
+            unit(outgoing_ref, there, part), unit(got, e, part), send.at[index], recv.at[e], target_id
+        )
+
+    barrier = pltpu.get_barrier_semaphore()
+    pl.semaphore_signal(barrier, inc=1, device_id=place.other_head(), device_id_type=MESH)
+    for step in order:
+        pl.semaphore_signal(
+            barrier, inc=1, device_id=(h, target(*step)), device_id_type=MESH
+        )
+    loads[0].wait()
+    for k in range(count * most):
+        outgoing_ref[k] = cache_ref[senders[k]]
+    own = pltpu.make_async_copy(unit(outgoing_ref, e), unit(got, e), own_sem)
+    own.start()
+    pl.semaphore_wait(barrier, count)
+
+    for index, step in enumerate(order):
+        there = target(*step)
+        sent(index, there, (h, there)).start()
+
+    def arrived(step, b):
+        part = positions(step)
+        remote(
+            unit(outgoing_ref, b, part), unit(got, b, part), send.at[0], recv.at[b], me
+        ).wait_recv()
+
+    def passed(index, b, head, target_id):
+        return remote(
+            unit(got, b, head), unit(got, b, head), pass_send.at[index], pass_recv.at[b], target_id
+        )
+
+    def resident(r):
+        scores_r = jnp.dot(queries_ref[r], resident_ref[r], preferred_element_type=jnp.float32)
+        weights = weigh(scores_r, resident_len[r])
+        latent_ref[r] = score(weights, resident_ref[r, :width, :]).astype(latent_ref.dtype)
+
+    own.wait()
+    loads[1].wait()
+    loads[2].wait()
+    crossing = [i for i in range(count - 1) if order[i][0] == 1]
+    inside = [i for i in range(count - 1) if order[i][0] == 0]
+    done = 0
+    for k, index in enumerate(crossing):
+        b = source(*order[index])
+        arrived(order[index], b)
+        passed(index, b, h, place.other_head()).start()
+        if k % 2 == 1 and done < req_count:
+            resident(done)
+            done += 1
+    for r in range(done, req_count):
+        resident(r)
+    for index in inside:
+        arrived(order[index], source(*order[index]))
+    for index in crossing:
+        b = source(*order[index])
+        passed(index, b, 1 - h, me).wait_recv()
+
+    def cache_of(j):
+        cache = got[slot[j]]
+        return cache.reshape(cache.shape[0] * cache.shape[1], cache.shape[2])
+
+    for j in range(new_count):
+        scores[j] = score(queries_ref[req_count + j], cache_of(j))
+    for j in range(new_count):
+        weights = weigh(scores[j], new_len[j])
+        latent_ref[req_count + j] = jnp.dot(
+            weights, cache_of(j)[:, :width], preferred_element_type=jnp.float32
+        ).astype(latent_ref.dtype)
+
+    for index, step in enumerate(order):
+        sent(index, target(*step), me).wait_send()
+    for index in crossing:
+        passed(index, source(*order[index]), h, me).wait_send()
+
+
+def latents(nz, most, cache, queries, resident, resident_len, senders, slot, new_len, width):
+    new_count, halves, piece, cache_width = cache.shape
+    rows, heads, _ = queries.shape
+    slots = senders.shape[0]
+    count = nz * 4
+    dma = pltpu.SemaphoreType.DMA
+    hbm = pl.BlockSpec(memory_space=pl.ANY)
+    smem = pl.BlockSpec(memory_space=pltpu.SMEM)
+    return pl.pallas_call(
+        functools.partial(handoff, nz, most),
+        out_shape=jax.ShapeDtypeStruct((rows, heads, width), jnp.bfloat16),
+        in_specs=[hbm, hbm, hbm, smem, smem, smem, smem],
+        out_specs=pl.BlockSpec(memory_space=pltpu.VMEM),
+        scratch_shapes=[
+            pltpu.VMEM(cache.shape, jnp.bfloat16),
+            pltpu.VMEM((slots,) + cache.shape[1:], jnp.bfloat16),
+            pltpu.VMEM(queries.shape, jnp.bfloat16),
+            pltpu.VMEM(resident.shape, jnp.bfloat16),
+            pltpu.VMEM((slots,) + cache.shape[1:], jnp.bfloat16),
+            pltpu.VMEM((new_count, heads, halves * piece), jnp.float32),
+            dma((3,)),
+            dma,
+            dma((count,)),
+            dma((count,)),
+            dma((count,)),
+            dma((count,)),
+        ],
+        compiler_params=pltpu.CompilerParams(
+            collective_id=1, has_side_effects=True, vmem_limit_bytes=62 * 2**20
+        ),
+        name="handoff",
+    )(cache, queries, resident, resident_len, senders, slot, new_len)
 
 
 def per_device(
@@ -623,56 +883,58 @@
         ),
         axis=1,
     )
-    share = lax.dynamic_slice_in_dim(new_cache, head_index * piece, piece, axis=1)
-    outgoing = jnp.take(share, senders, axis=0, mode="clip").reshape(
-        n_expert, most, piece, cache_width
-    )
-    incoming = lax.all_to_all(outgoing, "expert", split_axis=0, concat_axis=0, tiled=True)
     position = jnp.arange(new_owner.shape[0], dtype=jnp.int32)
     named = new_owner == owner_index
     before = jnp.sum((named[None, :] & (position[None, :] < position[:, None])).astype(jnp.int32), 1)
-    chosen = jnp.sum(
-        jnp.where(
-            named[None, :]
-            & (before[None, :] == jnp.arange(new_count, dtype=jnp.int32)[:, None]),
-            position[None, :],
-            0,
-        ),
-        axis=1,
-    )
+    taken = named[None, :] & (
+        before[None, :] == jnp.arange(new_count, dtype=jnp.int32)[:, None]
+    )
+    chosen = jnp.sum(jnp.where(taken, position[None, :], 0), axis=1)
     anchor = chosen // new_count
-    arrived_share = jnp.take(
-        incoming.reshape(n_expert * most, piece, cache_width),
-        anchor * most + earlier_equal(anchor),
-        axis=0,
-        mode="clip",
-    )
-    if n_head == 2:
-        other = lax.ppermute(arrived_share, "head", [(0, 1), (1, 0)])
-        first = jnp.where(head_index == 0, arrived_share, other)
-        last = jnp.where(head_index == 0, other, arrived_share)
-        arrived = jnp.concatenate([first, last], axis=1)
-    else:
-        arrived = lax.all_gather(arrived_share, "head", axis=1, tiled=True)
-    resident_att = attend(queries[:req_count], resident_cache, resident_len, value_up)
-    arrived_att = attend(queries[req_count:], arrived, new_len[chosen], value_up)
-    attention = jnp.concatenate([resident_att, arrived_att], axis=0)
-
-    if n_head == 2 and n_expert % 4 == 0 and local_experts == 1:
-        mine = expert_ids == owner_index
-        weight = jnp.sum(jnp.where(mine, expert_gates, 0.0), axis=1, keepdims=True)
+    slot = anchor * most + earlier_equal(anchor)
+    lengths = jnp.sum(jnp.where(taken, new_len[None, :], 0), axis=1)
+
+    if n_head == 2 and n_expert % 8 == 0 and local_experts == 1:
+        latent = latents(
+            n_expert // 4,
+            most,
+            new_cache.reshape(new_count, n_head, piece, cache_width),
+            queries,
+            jnp.swapaxes(resident_cache, 1, 2),
+            resident_len,
+            senders,
+            slot,
+            lengths,
+            value_up.shape[1],
+        )
+        attention = jnp.einsum(
+            "rhc,hcv->hrv", latent, value_up, preferred_element_type=jnp.float32
+        ).astype(jnp.bfloat16)
         return fused_layer(
             n_expert // 4,
             attention,
             w_output.T,
-            residual,
+            residual.T,
             norm_gain.reshape(n_expert, 1, -1),
-            weight,
+            expert_ids.T,
+            expert_gates.T,
             w_gate[0],
             w_up[0],
             w_down[0],
         )
 
+    share = lax.dynamic_slice_in_dim(new_cache, head_index * piece, piece, axis=1)
+    outgoing = jnp.take(share, senders, axis=0, mode="clip").reshape(
+        n_expert, most, piece, cache_width
+    )
+    incoming = lax.all_to_all(outgoing, "expert", split_axis=0, concat_axis=0, tiled=True)
+    arrived_share = jnp.take(
+        incoming.reshape(n_expert * most, piece, cache_width), slot, axis=0, mode="clip"
+    )
+    arrived = lax.all_gather(arrived_share, "head", axis=1, tiled=True)
+    resident_att = attend(queries[:req_count], resident_cache, resident_len, value_up)
+    arrived_att = attend(queries[req_count:], arrived, lengths, value_up)
+    attention = jnp.concatenate([resident_att, arrived_att], axis=0)
     mixed = jnp.dot(
         lax.all_gather(attention, "expert", axis=0, tiled=True),
         w_output,

time: 169 us -> 158 us (0.935)
  Pallas kernels: 106 us -> 144 us
  waiting for transfers between devices: 27.4 us -> 0 us
  starting transfers between devices: 9.11 us -> 0 us
  matrix products: 14.5 us -> 6.05 us
  local copies, waits for them, and re-layouts: 8.26 us -> 3.14 us
  other arithmetic: 2.72 us -> 4.45 us
    pallas_call x1 -> x2, Pallas kernels: 106 us -> 144 us  [the longest x1 99.5 us: fused_layer(): pl.pallas_call(functools.partial(layer, nz, plain_rows, n_early), out_sha...]
    all_to_all x1 -> x0, waiting for transfers between devices: 20 us -> none  [per_device(): lax.all_to_all(outgoing, 'expert', split_axis=0, concat_axis=0, tiled=True)]
    dot_general x6 -> x1, matrix products: 14.5 us -> 6.05 us  [per_device(): jnp.einsum('rhc,hcv->hrv', latent, value_up, preferred_element_type=jnp.f...]
    all_to_all x1 -> x0, starting transfers between devices: 7.56 us -> none  [per_device(): lax.all_to_all(outgoing, 'expert', split_axis=0, concat_axis=0, tiled=True)]
    ppermute x1 -> x0, waiting for transfers between devices: 7.36 us -> none  [per_device(): other = lax.ppermute(arrived_share, 'head', [(0, 1), (1, 0)])]
    gather x3 -> x0, local copies, waits for them, and re-layouts: 3.06 us -> none  [the longest x1 1.76 us: per_device(): jnp.take(share, senders, axis=0, mode='clip')]
  transfers between devices with their start and end apart: 2 -> 0, of which waited for: 2 -> 0; matrix products, arithmetic and copies ran while one was open for 7% -> 0% of each run, Pallas kernels for 0% -> 0%
where the time goes in v2:
time: 158 us
  Pallas kernels  144 us (91%)
  matrix products  6.05 us (4%)
  other arithmetic  4.45 us (3%)
  local copies, waits for them, and re-layouts  3.14 us (2%)
    pallas_call x1, Pallas kernels, fused_layer(): pl.pallas_call(functools.partial(layer, nz, plain_rows, n_early), out_sha...  99.5 us
    pallas_call x1, Pallas kernels, latents(): pl.pallas_call(functools.partial(handoff, nz, most), out_shape=jax.ShapeD...  44.4 us
    dot_general x1, matrix products, per_device(): jnp.einsum('rhc,hcv->hrv', latent, value_up, preferred_element_type=jnp.f...  6.05 us

profile of v2, /device:TPU:0, one launch (start us, length us, event | category | flops | bytes accessed | tf_op | source)
XLA Modules:
  0.0 157.6 jit_solution(16911747415965697840)
XLA Ops:
  0.0 0.0 copy-start
  0.0 0.8 dynamic_slice.3
  0.8 0.2 convert_reduce_fusion.2
  1.0 0.8 multiply_add_fusion.1
  1.7 0.6 select_reduce_fusion.2.senders
  2.3 0.7 broadcast_compare_fusion
  3.0 0.1 convert_reduce_fusion
  3.1 1.4 select_reduce_fusion
  4.5 0.2 convert_reduce_fusion.1
  4.7 0.5 multiply_add_fusion.slot
  5.2 44.4 %handoff.1 = bf16[16,64,512]{2,1,0:T(8,128)(2,1)} custom-call(bf16[12,2,32,576]{3,2,1,0:T(8,128)(2,1)} %bitcast.15, bf16[16,64,576]{2,1,0:T(8,128)(2,1)} %queries_hbm.1, bf16[4,576,256]{2,1,0:T(8,128)(2,1)} %bitcast.14, s32[4]{0:T(128)} %resident_len.1, s32[32]{0:T(128)} %select_reduce_fusion.2.senders, s32[12]{0:T(128)} %multiply_add_fusion.slot, ...), custom_call_target="tpu_custom_call" | custom-call | tf_op jit(solution)/shard_map/handoff/pallas_call | solution.py:821
  49.6 6.0 %convolution_convert_fusion.att_ref = bf16[64,16,128]{2,1,0:T(8,128)(2,1)} fusion(bf16[64,512,128]{2,1,0:T(8,128)(2,1)} %param.21, bf16[16,64,512]{2,1,0:T(8,128)(2,1)} %handoff.1), kind=kOutput, calls=%fused_computation | convolution fusion | flops 134348800 | bytes 9699328 | tf_op jit(solution)/shard_map/rhc,hcv->hrv/dot_general | solution.py:910
  55.7 0.0 copy-done
  55.7 0.7 reshape.34.gain_ref
  56.4 99.5 %fused_layer.1 = bf16[128,448]{1,0:T(8,128)(2,1)} custom-call(bf16[64,16,128]{2,1,0:T(8,128)(2,1)} %convolution_convert_fusion.att_ref, bf16[448,256]{1,0:T(8,128)(2,1)} %bitcast.16, bf16[16,1,448]{2,1,0:T(2,128)(2,1)} %reshape.34.gain_ref, s32[8,256]{1,0:T(8,128)} %bitcast.17, f32[8,256]{1,0:T(8,128)} %bitcast.18, bf16[448,8192]{1,0:T(8,128)(2,1)} %bitcast.10, ...), custom_call_target="tpu_custom_call" | custom-call | tf_op jit(solution)/shard_map/fused_layer/pallas_call | solution.py:587
  155.9 1.7 %copy.23 = bf16[128,448]{0,1:T(8,128)(2,1)} copy(bf16[128,448]{1,0:T(8,128)(2,1)} %fused_layer.1) | data formatting | bytes 229376 | tf_op jit(solution)/shard_map/fused_layer/pallas_call | solution.py:587
  (1 shorter events, 0.0 us)
Async XLA Ops:
  0.0 55.7 %copy-start = (bf16[7168]{0:T(1024)(128)(2,1)S(1)}, bf16[7168]{0:T(1024)(128)(2,1)}, u32[]{:S(2)}) copy-start(bf16[7168]{0:T(1024)(128)(2,1)} %param.26) | copy-start | bytes 43012

commit v3 on v2

--- a/solution.py
+++ b/solution.py
@@ -396,27 +396,23 @@
 
     settle_hidden = gather(place, hidden_view, [0, 1 + h], (1,), (h_z, h_y, h_c, h_x, h_recv))
 
-    def square(b, total):
-        values = hidden[b].astype(f32)
-        return total + jnp.sum(values * values, axis=1, keepdims=True)
-
-    squares = lax.fori_loop(0, blocks, square, jnp.zeros((rows, 1), f32))
-    inverse = lax.rsqrt(squares * (1.0 / (blocks * width)) + 1e-06)
     loads[1].wait()
     loads[2].wait()
     gate_acc[...] = jnp.zeros_like(gate_acc)
     up_acc[...] = jnp.zeros_like(up_acc)
 
-    def raise_up(b, carry):
-        normed = (hidden[b].astype(f32) * inverse * gain_ref[b].astype(f32)).astype(bf16)
+    def raise_up(b, squares):
+        values = hidden[b].astype(f32)
+        scaled = (values * gain_ref[b].astype(f32)).astype(bf16)
         at = pl.ds(pl.multiple_of(b * width, 64), width)
-        gate_acc[...] += jnp.dot(normed, wg[at, :], preferred_element_type=f32)
-        up_acc[...] += jnp.dot(normed, wu[at, :], preferred_element_type=f32)
-        return carry
-
-    lax.fori_loop(0, blocks, raise_up, 0)
-    gate = gate_acc[...]
-    act[...] = (jax.nn.silu(gate) * up_acc[...] * weight).astype(bf16)
+        gate_acc[...] += jnp.dot(scaled, wg[at, :], preferred_element_type=f32)
+        up_acc[...] += jnp.dot(scaled, wu[at, :], preferred_element_type=f32)
+        return squares + jnp.sum(values * values, axis=1, keepdims=True)
+
+    squares = lax.fori_loop(0, blocks, raise_up, jnp.zeros((rows, 1), f32))
+    inverse = lax.rsqrt(squares * (1.0 / (blocks * width)) + 1e-06)
+    gate = gate_acc[...] * inverse
+    act[...] = (jax.nn.silu(gate) * up_acc[...] * (inverse * weight)).astype(bf16)
     loads[3].wait()
 
     pair_width = 2 * width
@@ -677,9 +673,11 @@
     latent_ref,
     cache_ref,
     outgoing_ref,
+    outgoing_tail,
     queries_ref,
     resident_ref,
     got,
+    got_tail,
     scores,
     load_sem,
     own_sem,
@@ -732,11 +730,19 @@
     def positions(step):
         return h if step[0] == 1 else None
 
+    def tail(ref, b, head=None):
+        return ref.at[b] if head is None else ref.at[b, head]
+
     def sent(index, there, target_id):
         part = positions(order[index])
-        return remote(
-            unit(outgoing_ref, there, part), unit(got, e, part), send.at[index], recv.at[e], target_id
-        )
+        return [
+            remote(
+                view(src, there, part), view(dst, e, part), send.at[k, index], recv.at[k, e], target_id
+            )
+            for k, (view, src, dst) in enumerate(
+                ((unit, outgoing_ref, got), (tail, outgoing_tail, got_tail))
+            )
+        ]
 
     barrier = pltpu.get_barrier_semaphore()
     pl.semaphore_signal(barrier, inc=1, device_id=place.other_head(), device_id_type=MESH)
@@ -745,33 +751,49 @@
             barrier, inc=1, device_id=(h, target(*step)), device_id_type=MESH
         )
     loads[0].wait()
-    for k in range(count * most):
-        outgoing_ref[k] = cache_ref[senders[k]]
-    own = pltpu.make_async_copy(unit(outgoing_ref, e), unit(got, e), own_sem)
-    own.start()
+    for b in range(count):
+        caches = [cache_ref[senders[b * most + k]] for k in range(most)]
+        for k in range(most):
+            outgoing_ref[b * most + k] = caches[k][:, :, :width]
+        outgoing_tail[b] = jnp.concatenate([cache[:, :, width:] for cache in caches], axis=2)
+    own = [
+        pltpu.make_async_copy(unit(outgoing_ref, e), unit(got, e), own_sem.at[0]),
+        pltpu.make_async_copy(outgoing_tail.at[e], got_tail.at[e], own_sem.at[1]),
+    ]
+    for copy in own:
+        copy.start()
     pl.semaphore_wait(barrier, count)
 
     for index, step in enumerate(order):
         there = target(*step)
-        sent(index, there, (h, there)).start()
+        for copy in sent(index, there, (h, there)):
+            copy.start()
 
     def arrived(step, b):
         part = positions(step)
-        remote(
-            unit(outgoing_ref, b, part), unit(got, b, part), send.at[0], recv.at[b], me
-        ).wait_recv()
+        for k, (view, ref) in enumerate(((unit, got), (tail, got_tail))):
+            at = view(ref, b, part)
+            remote(at, at, send.at[k, 0], recv.at[k, b], me).wait_recv()
 
     def passed(index, b, head, target_id):
-        return remote(
-            unit(got, b, head), unit(got, b, head), pass_send.at[index], pass_recv.at[b], target_id
-        )
+        return [
+            remote(
+                view(ref, b, head),
+                view(ref, b, head),
+                pass_send.at[k, index],
+                pass_recv.at[k, b],
+                target_id,
+            )
+            for k, (view, ref) in enumerate(((unit, got), (tail, got_tail)))
+        ]
 
     def resident(r):
         scores_r = jnp.dot(queries_ref[r], resident_ref[r], preferred_element_type=jnp.float32)
         weights = weigh(scores_r, resident_len[r])
         latent_ref[r] = score(weights, resident_ref[r, :width, :]).astype(latent_ref.dtype)
 
-    own.wait()
+    for copy in own:
+        copy.wait()
     loads[1].wait()
     loads[2].wait()
     crossing = [i for i in range(count - 1) if order[i][0] == 1]
@@ -780,7 +802,8 @@
     for k, index in enumerate(crossing):
         b = source(*order[index])
         arrived(order[index], b)
-        passed(index, b, h, place.other_head()).start()
+        for copy in passed(index, b, h, place.other_head()):
+            copy.start()
         if k % 2 == 1 and done < req_count:
             resident(done)
             done += 1
@@ -790,24 +813,40 @@
         arrived(order[index], source(*order[index]))
     for index in crossing:
         b = source(*order[index])
-        passed(index, b, 1 - h, me).wait_recv()
+        for copy in passed(index, b, 1 - h, me):
+            copy.wait_recv()
+
+    def flat(cache):
+        return cache.reshape(cache.shape[0] * cache.shape[1], cache.shape[2])
 
     def cache_of(j):
-        cache = got[slot[j]]
-        return cache.reshape(cache.shape[0] * cache.shape[1], cache.shape[2])
+        return flat(got[slot[j]])
+
+    def tail_of(j):
+        tails = flat(got_tail[slot[j] // most])
+        length = tails.shape[1] // most
+        chosen = tails[:, :length]
+        for k in range(1, most):
+            chosen = jnp.where(slot[j] % most == k, tails[:, k * length : (k + 1) * length], chosen)
+        return chosen
 
     for j in range(new_count):
-        scores[j] = score(queries_ref[req_count + j], cache_of(j))
+        own_queries = queries_ref[req_count + j]
+        scores[j] = score(own_queries[:, :width], cache_of(j)) + score(
+            own_queries[:, width:], tail_of(j)
+        )
     for j in range(new_count):
         weights = weigh(scores[j], new_len[j])
         latent_ref[req_count + j] = jnp.dot(
-            weights, cache_of(j)[:, :width], preferred_element_type=jnp.float32
+            weights, cache_of(j), preferred_element_type=jnp.float32
         ).astype(latent_ref.dtype)
 
     for index, step in enumerate(order):
-        sent(index, target(*step), me).wait_send()
+        for copy in sent(index, target(*step), me):
+            copy.wait_send()
     for index in crossing:
-        passed(index, source(*order[index]), h, me).wait_send()
+        for copy in passed(index, source(*order[index]), h, me):
+            copy.wait_send()
 
 
 def latents(nz, most, cache, queries, resident, resident_len, senders, slot, new_len, width):
@@ -825,17 +864,19 @@
         out_specs=pl.BlockSpec(memory_space=pltpu.VMEM),
         scratch_shapes=[
             pltpu.VMEM(cache.shape, jnp.bfloat16),
-            pltpu.VMEM((slots,) + cache.shape[1:], jnp.bfloat16),
+            pltpu.VMEM((slots, halves, piece, width), jnp.bfloat16),
+            pltpu.VMEM((count, halves, piece, most * (cache_width - width)), jnp.bfloat16),
             pltpu.VMEM(queries.shape, jnp.bfloat16),
             pltpu.VMEM(resident.shape, jnp.bfloat16),
-            pltpu.VMEM((slots,) + cache.shape[1:], jnp.bfloat16),
+            pltpu.VMEM((slots, halves, piece, width), jnp.bfloat16),
+            pltpu.VMEM((count, halves, piece, most * (cache_width - width)), jnp.bfloat16),
             pltpu.VMEM((new_count, heads, halves * piece), jnp.float32),
             dma((3,)),
-            dma,
-            dma((count,)),
-            dma((count,)),
-            dma((count,)),
-            dma((count,)),
+            dma((2,)),
+            dma((2, count)),
+            dma((2, count)),
+            dma((2, count)),
+            dma((2, count)),
         ],
         compiler_params=pltpu.CompilerParams(
             collective_id=1, has_side_effects=True, vmem_limit_bytes=62 * 2**20

time: 158 us -> 153 us (0.968)
  Pallas kernels: 144 us -> 139 us
    pallas_call x1, Pallas kernels: 99.5 us -> 97.3 us  [fused_layer(): pl.pallas_call(functools.partial(layer, nz, plain_rows, n_early), out_sha...]
    pallas_call x1, Pallas kernels: 44.4 us -> 42.2 us  [latents(): pl.pallas_call(functools.partial(handoff, nz, most), out_shape=jax.ShapeD...]
where the time goes in v3:
time: 153 us
  Pallas kernels  139 us (91%)
  matrix products  6.05 us (4%)
  other arithmetic  4.45 us (3%)
  local copies, waits for them, and re-layouts  3.14 us (2%)
    pallas_call x1, Pallas kernels, fused_layer(): pl.pallas_call(functools.partial(layer, nz, plain_rows, n_early), out_sha...  97.3 us
    pallas_call x1, Pallas kernels, latents(): pl.pallas_call(functools.partial(handoff, nz, most), out_shape=jax.ShapeD...  42.2 us
    dot_general x1, matrix products, per_device(): jnp.einsum('rhc,hcv->hrv', latent, value_up, preferred_element_type=jnp.f...  6.05 us

profile of v3, /device:TPU:0, one launch (start us, length us, event | category | flops | bytes accessed | tf_op | source)
XLA Modules:
  0.0 153.1 jit_solution(15312855732423212519)
XLA Ops:
  0.0 0.0 copy-start
  0.0 0.8 dynamic_slice.3
  0.8 0.2 convert_reduce_fusion.2
  1.0 0.8 multiply_add_fusion.1
  1.7 0.6 select_reduce_fusion.2.senders
  2.3 0.7 broadcast_compare_fusion
  3.0 0.1 convert_reduce_fusion
  3.1 1.4 select_reduce_fusion
  4.5 0.2 convert_reduce_fusion.1
  4.7 0.5 multiply_add_fusion.slot
  5.2 42.2 %handoff.1 = bf16[16,64,512]{2,1,0:T(8,128)(2,1)} custom-call(bf16[12,2,32,576]{3,2,1,0:T(8,128)(2,1)} %bitcast.15, bf16[16,64,576]{2,1,0:T(8,128)(2,1)} %queries_hbm.1, bf16[4,576,256]{2,1,0:T(8,128)(2,1)} %bitcast.14, s32[4]{0:T(128)} %resident_len.1, s32[32]{0:T(128)} %select_reduce_fusion.2.senders, s32[12]{0:T(128)} %multiply_add_fusion.slot, ...), custom_call_target="tpu_custom_call" | custom-call | tf_op jit(solution)/shard_map/handoff/pallas_call | solution.py:860
  47.4 6.0 %convolution_convert_fusion.att_ref = bf16[64,16,128]{2,1,0:T(8,128)(2,1)} fusion(bf16[64,512,128]{2,1,0:T(8,128)(2,1)} %param.21, bf16[16,64,512]{2,1,0:T(8,128)(2,1)} %handoff.1), kind=kOutput, calls=%fused_computation | convolution fusion | flops 134348800 | bytes 9699328 | tf_op jit(solution)/shard_map/rhc,hcv->hrv/dot_general | solution.py:951
  53.5 0.0 copy-done
  53.5 0.7 reshape.34.gain_ref
  54.2 97.3 %fused_layer.1 = bf16[128,448]{1,0:T(8,128)(2,1)} custom-call(bf16[64,16,128]{2,1,0:T(8,128)(2,1)} %convolution_convert_fusion.att_ref, bf16[448,256]{1,0:T(8,128)(2,1)} %bitcast.16, bf16[16,1,448]{2,1,0:T(2,128)(2,1)} %reshape.34.gain_ref, s32[8,256]{1,0:T(8,128)} %bitcast.17, f32[8,256]{1,0:T(8,128)} %bitcast.18, bf16[448,8192]{1,0:T(8,128)(2,1)} %bitcast.10, ...), custom_call_target="tpu_custom_call" | custom-call | tf_op jit(solution)/shard_map/fused_layer/pallas_call | solution.py:583
  151.5 1.7 %copy.23 = bf16[128,448]{0,1:T(8,128)(2,1)} copy(bf16[128,448]{1,0:T(8,128)(2,1)} %fused_layer.1) | data formatting | bytes 229376 | tf_op jit(solution)/shard_map/fused_layer/pallas_call | solution.py:583
  (1 shorter events, 0.0 us)
Async XLA Ops:
  0.0 53.5 %copy-start = (bf16[7168]{0:T(1024)(128)(2,1)S(1)}, bf16[7168]{0:T(1024)(128)(2,1)}, u32[]{:S(2)}) copy-start(bf16[7168]{0:T(1024)(128)(2,1)} %param.26) | copy-start | bytes 43012
